TPU v7x, 32 devices: a whole 2x2x4 slice. The times are simulated.
32 devices in a mesh: gx: 4 (over y, x), gy: 8 (over z, core).
Axes of the slice: x: 2, y: 2, z: 4, core: 2. Of those that a mesh axis runs over, the one named last changes fastest.
Arguments:
- basis_fields: float32 [128, 128, 1024], P(None, 'gx', 'gy'), may hold values from -6 to 6
- carried_fields: float32 [128, 128, 1024], P(None, 'gx', 'gy'), may hold values from -70 to 70, as said below
- velocity: float32 [2, 128, 1024], P(None, 'gx', 'gy'), may hold values from -1 to 1
- diffusion: float32 [128, 128], replicated, may hold values from -0.024 to 0.09, as said below
- advection: float32 [128, 128], replicated, may hold values from -0.18 to 0.18
Outputs:
- new_basis: float32 [256, 128, 1024], P(None, 'gx', 'gy')
- galerkin: float32 [256, 128], replicated
Inputs may be any that keep to these rules, and one draw needn't show every extreme that they name: `carried_fields`: entries of the field block are of order one with scales varying over cells and fields. `diffusion`: A positive diagonal with small couplings off it.
All inputs are finite; a program needn't handle non-finite values.
Results may differ from a plain program's by a relative error of at most 0.000086.
Values sent between devices are 32-bit elements; how exact they have to be, the bound alone decides.
No kernel may reach another device: no remote copies, remote signals or barrier semaphores. Data moves between devices by JAX's collectives and lax.ppermute only.
A program may use at most 64 MiB of HBM per device.

v0:
```python
import functools
import jax
import jax.numpy as jnp
from jax import lax
from jax.experimental import pallas as pl
from jax.experimental.pallas import tpu as pltpu
from jax.sharding import PartitionSpec as P


def neighbour(array, axis, step):
    count = lax.axis_size(axis)
    pairs = [(i, (i + step) % count) for i in range(count)]
    return lax.ppermute(array, axis, pairs)


def keep_edges(r, block, top_ref, bottom_ref, first_ref, last_ref, rows, cols):
    if r == 0:
        top_ref[...] = block
    if r == rows - 1:
        bottom_ref[...] = block
    first_ref[:, r:r + 1] = block[:, 0:1]
    last_ref[:, r:r + 1] = block[:, cols - 1:cols]


def edges_kernel(f_ref, top_ref, bottom_ref, first_ref, last_ref, *, count, rows, cols):
    for r in range(rows):
        block = f_ref[pl.ds(r, count, stride=rows), :]
        keep_edges(r, block, top_ref, bottom_ref, first_ref, last_ref, rows, cols)


def substep_kernel(f_ref, above_ref, below_ref, left_ref, right_ref, vel_ref, mix_ref, out_ref,
                   top_ref, bottom_ref, first_ref, last_ref, *, count, rows, cols):
    col_id = lax.broadcasted_iota(jnp.int32, (count, cols), 1)
    coupling = mix_ref[...]

    def row_of(r):
        if r < 0:
            return above_ref[...]
        if r >= rows:
            return below_ref[...]
        return f_ref[pl.ds(r, count, stride=rows), :]

    prev, here = row_of(-1), row_of(0)
    for r in range(rows):
        nxt = row_of(r + 1)
        west = left_ref[:, r:r + 1]
        east = right_ref[:, r:r + 1]
        minus_y = jnp.where(col_id == 0, west, pltpu.roll(here, 1, 1))
        plus_y = jnp.where(col_id == cols - 1, east, pltpu.roll(here, cols - 1, 1))
        speed_x = vel_ref[r:r + 1, :]
        speed_y = vel_ref[rows + r:rows + r + 1, :]
        laplace = nxt + prev + plus_y + minus_y - 4.0 * here
        transport = speed_x * (nxt - prev) * 0.5 + speed_y * (plus_y - minus_y) * 0.5
        rate = jnp.dot(coupling, jnp.concatenate([laplace, transport], 0),
                       precision=lax.Precision.HIGHEST, preferred_element_type=jnp.float32)
        result = here + rate
        out_ref[pl.ds(r, count, stride=rows), :] = result
        keep_edges(r, result, top_ref, bottom_ref, first_ref, last_ref, rows, cols)
        prev, here = here, nxt


def edge_shapes(count, rows, cols):
    return [
        jax.ShapeDtypeStruct((count, cols), jnp.float32),
        jax.ShapeDtypeStruct((count, cols), jnp.float32),
        jax.ShapeDtypeStruct((count, rows), jnp.float32),
        jax.ShapeDtypeStruct((count, rows), jnp.float32),
    ]


def edges_call(flat, count, rows, cols):
    vmem = pl.BlockSpec(memory_space=pltpu.VMEM)
    return pl.pallas_call(
        functools.partial(edges_kernel, count=count, rows=rows, cols=cols),
        out_shape=edge_shapes(count, rows, cols),
        in_specs=[vmem],
        out_specs=[vmem] * 4,
    )(flat)


def substep_call(flat, above, below, left, right, vel, coupling, count, rows, cols):
    vmem = pl.BlockSpec(memory_space=pltpu.VMEM)
    return pl.pallas_call(
        functools.partial(substep_kernel, count=count, rows=rows, cols=cols),
        out_shape=[jax.ShapeDtypeStruct((count * rows, cols), jnp.float32)]
        + edge_shapes(count, rows, cols),
        in_specs=[vmem] * 7,
        out_specs=[vmem] * 5,
    )(flat, above, below, left, right, vel, coupling)


def one_substep(flat, edges, flat_velocity, coupling, count, rows, cols):
    top, bottom, first, last = edges
    above = neighbour(bottom, "gx", 1)
    below = neighbour(top, "gx", -1)
    left = neighbour(last, "gy", 1)
    right = neighbour(first, "gy", -1)
    result = substep_call(flat, above, below, left, right, flat_velocity, coupling, count, rows, cols)
    return result[0], result[1:]


def exchange_sum(array, axes):
    for axis in axes:
        count, stride = lax.axis_size(axis), 1
        while stride < count:
            pairs = [(i, i ^ stride) for i in range(count)]
            array = array + lax.ppermute(array, axis, pairs)
            stride *= 2
    return array


def hdot(a, b):
    return jnp.dot(a, b, precision=lax.Precision.HIGHEST)


def lower_inverse(matrix):
    low = jnp.linalg.cholesky(matrix)
    identity = jnp.eye(matrix.shape[0], dtype=matrix.dtype)
    return jax.scipy.linalg.solve_triangular(low, identity, lower=True)


def body(basis_fields, carried_fields, velocity, diffusion, advection):
    basis_rank, tile_rows, tile_cols = carried_fields.shape
    tile_cells = tile_rows * tile_cols
    aug_count = 2 * basis_rank
    cell_weight = 1.0 / (tile_cells * lax.axis_size("gx") * lax.axis_size("gy"))
    axes = ("gy", "gx")
    flat_basis = basis_fields.reshape(basis_rank, tile_cells)
    flat_carried = carried_fields.reshape(basis_rank, tile_cells)
    known = jnp.concatenate([flat_basis, flat_carried], 0)
    basis_sum = exchange_sum(hdot(flat_basis, known.T), axes) * cell_weight
    flat_velocity = velocity.reshape(2 * tile_rows, tile_cols)
    coupling = jnp.concatenate([diffusion.T, -advection.T], 1)
    shape = (basis_rank, tile_rows, tile_cols)
    carried_rows = carried_fields.reshape(basis_rank * tile_rows, tile_cols)
    edges = edges_call(carried_rows, *shape)
    section_one, edges = one_substep(carried_rows, edges, flat_velocity, coupling, *shape)
    section_two, _ = one_substep(section_one, edges, flat_velocity, coupling, *shape)
    flat_new = section_two.reshape(basis_rank, tile_cells)
    every = jnp.concatenate([flat_basis, flat_new, flat_carried], 0)
    new_sum = exchange_sum(hdot(flat_new, every.T), axes) * cell_weight
    inverse_11 = lower_inverse(basis_sum[:, :basis_rank])
    low_21 = hdot(new_sum[:, :basis_rank], inverse_11.T)
    schur = new_sum[:, basis_rank:aug_count] - hdot(low_21, low_21.T)
    inverse_22 = lower_inverse(schur)
    top = hdot(inverse_11, flat_basis)
    bottom = hdot(inverse_22, flat_new - hdot(low_21, top))
    new_basis = jnp.concatenate([top, bottom], 0)
    galerkin_top = hdot(inverse_11, basis_sum[:, basis_rank:])
    galerkin_bottom = hdot(inverse_22, new_sum[:, aug_count:] - hdot(low_21, galerkin_top))
    galerkin = jnp.concatenate([galerkin_top, galerkin_bottom], 0)
    return (new_basis.reshape(aug_count, tile_rows, tile_cols), galerkin)


def solution(mesh):
    in_specs = (P(None, "gx", "gy"), P(None, "gx", "gy"), P(None, "gx", "gy"), P(), P())
    out_specs = (P(None, "gx", "gy"), P())
    return jax.shard_map(body, mesh=mesh, in_specs=in_specs, out_specs=out_specs, check_vma=False)
```

profile of v0, /device:TPU:0, one launch (start us, length us, event | category | flops | bytes accessed | tf_op | source)
XLA Modules:
  0.0 150.6 jit_solution(4426375300776995682)
XLA Ops:
  0.6 4.3 %shard_map.68 = (f32[128,128]{1,0:T(8,128)}, f32[128,128]{1,0:T(8,128)}, f32[128,32]{1,0:T(8,128)}, f32[128,32]{1,0:T(8,128)}) custom-call(f32[4096,128]{1,0:T(8,128)} %bitcast.51), custom_call_target="tpu_custom_call" | custom-call | tf_op jit(solution)/shard_map/pallas_call | solution.py:73
  4.9 2.9 %collective-permute-start.5 = (f32[128,128]{1,0:T(8,128)}, f32[128,128]{1,0:T(8,128)S(1)}, u32[]{:S(2)}, u32[]{:S(2)}) collective-permute-start(f32[128,128]{1,0:T(8,128)} %get-tuple-element.14), channel_id=1, source_target_pairs={{0,8},{8,16},{16,24},{24,0},{1,9},{9,17},{17,25},{25,1},{2,10},{10... | collective-permute-start | bytes 196616 | tf_op jit(solution)/shard_map/ppermute | solution.py:13
  7.9 1.0 collective-permute-start.6
  8.8 4.0 %collective-permute-start.8 = (f32[128,32]{1,0:T(8,128)}, f32[128,32]{1,0:T(8,128)S(1)}, u32[]{:S(2)}, u32[]{:S(2)}) collective-permute-start(f32[128,32]{1,0:T(8,128)} %get-tuple-element.17), channel_id=1, source_target_pairs={{0,7},{1,0},{2,1},{3,2},{4,3},{5,4},{6,5},{7,6},{8,15},{9,8},{10,9... | collective-permute-start | bytes 49160 | tf_op jit(solution)/shard_map/ppermute | solution.py:13
  12.8 1.7 %copy.22 = f32[16,8,32,128]{3,1,2,0:T(8,128)S(1)} copy(f32[16,8,32,128]{3,2,1,0:T(8,128)S(1)} %bitcast.53) | data formatting | bytes 4194304
  14.5 1.6 %copy.23 = f32[16,8,32,128]{3,1,2,0:T(8,128)S(1)} copy(f32[16,8,32,128]{3,2,1,0:T(8,128)S(1)} %bitcast.55) | data formatting | bytes 4194304
  16.2 3.4 %fusion.10 = f32[128,256]{0,1:T(8,128)S(1)} fusion(f32[128,4096]{1,0:T(8,128)S(1)} %bitcast.58, f32[128,4096]{1,0:T(8,128)S(1)} %bitcast.56), kind=kOutput, calls=%fused_computation.14 | convolution fusion | flops 1611661312 | bytes 4325376 | tf_op jit(solution)/shard_map/dot_general | solution.py:113
  19.6 0.1 collective-permute-start
  19.7 0.1 copy.9
  19.8 0.1 copy.8
  19.9 0.7 pad_maximum_fusion.mix_ref
  20.7 0.6 copy-done.7
  21.3 0.1 copy-done.8
  21.3 0.0 copy-done.5
  21.3 0.0 copy-done.6
  21.3 10.1 %shard_map.69 = (f32[4096,128]{1,0:T(8,128)}, f32[128,128]{1,0:T(8,128)}, f32[128,128]{1,0:T(8,128)}, f32[128,32]{1,0:T(8,128)}, f32[128,32]{1,0:T(8,128)}) custom-call(f32[4096,128]{1,0:T(8,128)} %bitcast.52, f32[128,128]{1,0:T(8,128)} %copy-done.5, f32[128,128]{1,0:T(8,128)} %copy-done.6, f32[128,32]{1,0:T(8,128)} %copy-done.7, f32[128,32]{1,0:T(8,128)} %copy-done.8, ...), custom_call_target="tpu_custom_call" | custom-call | tf_op jit(solution)/shard_map/pallas_call | solution.py:83
  31.4 1.1 collective-permute-start.9
  32.5 1.9 %collective-permute-start.10 = (f32[128,128]{1,0:T(8,128)}, f32[128,128]{1,0:T(8,128)S(1)}, u32[]{:S(2)}, u32[]{:S(2)}) collective-permute-start(f32[128,128]{1,0:T(8,128)} %get-tuple-element.20), channel_id=1, source_target_pairs={{0,24},{8,0},{16,8},{24,16},{1,25},{9,1},{17,9},{25,17},{2,26},{10... | collective-permute-start | bytes 196616 | tf_op jit(solution)/shard_map/ppermute | solution.py:13
  34.3 3.5 %collective-permute-start.12 = (f32[128,32]{1,0:T(8,128)}, f32[128,32]{1,0:T(8,128)S(1)}, u32[]{:S(2)}, u32[]{:S(2)}) collective-permute-start(f32[128,32]{1,0:T(8,128)} %get-tuple-element.22), channel_id=1, source_target_pairs={{0,7},{1,0},{2,1},{3,2},{4,3},{5,4},{6,5},{7,6},{8,15},{9,8},{10,9... | collective-permute-start | bytes 49160 | tf_op jit(solution)/shard_map/ppermute | solution.py:13
  37.9 2.3 %collective-permute-done.11.left_ref = f32[128,32]{1,0:T(8,128)S(1)} collective-permute-done((f32[128,32]{1,0:T(8,128)}, f32[128,32]{1,0:T(8,128)S(1)}, u32[]{:S(2)}, u32[]{:S(2)}) %collective-permute-start.11) | collective-permute-done | bytes 16416 | tf_op jit(solution)/shard_map/ppermute | solution.py:13
  40.2 0.6 copy-done.11
  40.8 0.0 copy-done.12
  40.8 0.0 copy-done.9
  40.8 0.0 copy-done.10
  40.8 9.9 %shard_map.70 = (f32[4096,128]{1,0:T(8,128)}, f32[128,128]{1,0:T(8,128)}, f32[128,128]{1,0:T(8,128)}, f32[128,32]{1,0:T(8,128)}, f32[128,32]{1,0:T(8,128)}) custom-call(f32[4096,128]{1,0:T(8,128)} %get-tuple-element.18.f_ref, f32[128,128]{1,0:T(8,128)} %copy-done.9, f32[128,128]{1,0:T(8,128)} %copy-done.10, f32[128,32]{1,0:T(8,128)} %copy-done.11, ...), custom_call_target="tpu_custom_call" | custom-call | tf_op jit(solution)/shard_map/pallas_call | solution.py:83
  50.8 1.7 %reshape.34 = f32[128,4096]{1,0:T(8,128)S(1)} reshape(f32[4096,128]{1,0:T(8,128)} %get-tuple-element.23) | data formatting | bytes 4194304 | tf_op jit(solution)/shard_map/reshape | solution.py:139
  52.6 0.1 collective-permute-start.1
  52.7 8.5 %fusion = f32[128,384]{0,1:T(8,128)S(1)} fusion(f32[128,4096]{1,0:T(8,128)S(1)} %reshape.34, f32[128,4096]{1,0:T(8,128)} %bitcast.57, f32[128,4096]{1,0:T(8,128)} %bitcast.59), kind=kOutput, calls=%fused_computation | convolution fusion | flops 2419064832 | bytes 6488064 | tf_op jit(solution)/shard_map/dot_general | solution.py:113
  61.2 0.1 collective-permute-start.13
  61.3 3.5 %collective-permute-start.2 = (f32[128,256]{0,1:T(8,128)S(1)}, f32[128,256]{0,1:T(8,128)S(1)}, u32[]{:S(2)}, u32[]{:S(2)}) collective-permute-start(f32[128,256]{0,1:T(8,128)S(1)} %add.40), channel_id=1, source_target_pairs={{0,4},{1,5},{2,6},{3,7},{4,0},{5,1},{6,2},{7,3},{8,12},{9,13},{10,... | collective-permute-start | bytes 393224 | tf_op jit(solution)/shard_map/ppermute | solution.py:107
  64.7 6.5 %collective-permute-done.2 = f32[128,256]{0,1:T(8,128)S(1)} collective-permute-done((f32[128,256]{0,1:T(8,128)S(1)}, f32[128,256]{0,1:T(8,128)S(1)}, u32[]{:S(2)}, u32[]{:S(2)}) %collective-permute-start.2) | collective-permute-done | bytes 131104 | tf_op jit(solution)/shard_map/ppermute | solution.py:107
  71.3 0.6 collective-permute-start.3
  71.9 0.3 collective-permute-start.14
  72.1 4.2 %collective-permute-done.3 = f32[128,256]{0,1:T(8,128)S(1)} collective-permute-done((f32[128,256]{0,1:T(8,128)S(1)}, f32[128,256]{0,1:T(8,128)S(1)}, u32[]{:S(2)}, u32[]{:S(2)}) %collective-permute-start.3) | collective-permute-done | bytes 131104 | tf_op jit(solution)/shard_map/ppermute | solution.py:107
  76.3 2.1 %collective-permute-start.4 = (f32[128,256]{0,1:T(8,128)S(1)}, f32[128,256]{0,1:T(8,128)S(1)}, u32[]{:S(2)}, u32[]{:S(2)}) collective-permute-start(f32[128,256]{0,1:T(8,128)S(1)} %add.42), channel_id=1, source_target_pairs={{0,16},{8,24},{16,0},{24,8},{1,17},{9,25},{17,1},{25,9},{2,18},{10... | collective-permute-start | bytes 393224 | tf_op jit(solution)/shard_map/ppermute | solution.py:107
  78.4 1.5 collective-permute-start.15
  79.9 1.4 collective-permute-done.4
  81.4 0.1 copy.7
  81.5 11.7 %cholesky.44 = f32[128,128]{1,0:T(8,128)S(1)} custom-call(f32[128,128]{1,0:T(8,128)S(1)} %fusion.27), custom_call_target="Cholesky" | custom-call | tf_op jit(solution)/shard_map/jit(cholesky)/cholesky | solution.py:117
  93.3 0.6 compare_reduce_fusion.1
  93.9 0.7 fusion.17
  94.6 9.8 %custom-call.6 = f32[1,128,128]{1,2,0:T(8,128)S(1)} custom-call(f32[1,128,128]{2,1,0:T(8,128)S(1)} %fusion.17), custom_call_target="InvertDiagBlocksLowerTriangular" | custom-call | tf_op jit(solution)/shard_map/jit(_solve_triangular)/triangular_solve | solution.py:119
  104.4 0.3 fusion.15
  104.7 0.6 collective-permute-start.16
  105.3 4.5 %fusion.30 = f32[128,4096]{1,0:T(8,128)S(1)} fusion(f32[128,128]{1,0:T(8,128)S(1)} %fusion.15, f32[16,8,32,128]{3,2,1,0:T(8,128)} %bitcast.54), kind=kOutput, calls=%fused_computation.49 | convolution fusion | flops 805306368 | bytes 4259840 | tf_op jit(solution)/shard_map/dot_general | solution.py:113
  109.8 0.6 collective-permute-done.16
  110.5 2.1 %collective-permute-start.17 = (f32[128,384]{0,1:T(8,128)S(1)}, f32[128,384]{0,1:T(8,128)S(1)}, u32[]{:S(2)}, u32[]{:S(2)}) collective-permute-start(f32[128,384]{0,1:T(8,128)S(1)} %add.47), channel_id=1, source_target_pairs={{0,16},{8,24},{16,0},{24,8},{1,17},{9,25},{17,1},{25,9},{2,18},{10... | collective-permute-start | bytes 589832 | tf_op jit(solution)/shard_map/ppermute | solution.py:107
  112.5 0.3 fusion.20
  112.8 3.4 %collective-permute-done.17 = f32[128,384]{0,1:T(8,128)S(1)} collective-permute-done((f32[128,384]{0,1:T(8,128)S(1)}, f32[128,384]{0,1:T(8,128)S(1)}, u32[]{:S(2)}, u32[]{:S(2)}) %collective-permute-start.17) | collective-permute-done | bytes 196640 | tf_op jit(solution)/shard_map/ppermute | solution.py:107
  116.2 0.3 fusion.22
  116.5 0.3 slice_subtract_fusion.2
  116.8 0.1 copy.13
  116.9 11.9 %cholesky.55 = f32[128,128]{1,0:T(8,128)S(1)} custom-call(f32[128,128]{1,0:T(8,128)S(1)} %fusion.25), custom_call_target="Cholesky" | custom-call | tf_op jit(solution)/shard_map/jit(cholesky)/cholesky | solution.py:117
  128.9 0.6 compare_reduce_fusion
  129.5 0.7 fusion.18
  130.2 9.8 %custom-call.7 = f32[1,128,128]{1,2,0:T(8,128)S(1)} custom-call(f32[1,128,128]{2,1,0:T(8,128)S(1)} %fusion.18), custom_call_target="InvertDiagBlocksLowerTriangular" | custom-call | tf_op jit(solution)/shard_map/jit(_solve_triangular)/triangular_solve | solution.py:119
  140.0 0.3 fusion.13
  140.3 3.5 %convolution_subtract_fusion = f32[128,4096]{1,0:T(8,128)S(1)} fusion(f32[128,4096]{1,0:T(8,128)} %copy-done.1, f32[128,128]{1,0:T(8,128)S(1)} %fusion.22, f32[128,4096]{1,0:T(8,128)S(1)} %fusion.30), kind=kOutput, calls=%fused_computation.6 | convolution fusion | flops 805830656 | bytes 6356992 | tf_op jit(solution)/shard_map/dot_general | solution.py:113
  143.8 1.9 %fusion.31 = f32[128,4096]{1,0:T(8,128)S(1)} fusion(f32[128,128]{1,0:T(8,128)S(1)} %fusion.13, f32[128,4096]{1,0:T(8,128)S(1)} %convolution_subtract_fusion), kind=kOutput, calls=%fused_computation.50 | convolution fusion | flops 805306368 | bytes 4259840 | tf_op jit(solution)/shard_map/dot_general | solution.py:113
  145.8 0.4 maximum_bitcast_fusion
  146.2 2.8 %copy.18 = f32[32,8,32,128]{3,2,1,0:T(8,128)} copy(f32[32,8,32,128]{3,1,2,0:T(8,128)S(1)} %maximum_bitcast_fusion) | data formatting | bytes 8388608
  148.9 0.3 fusion.32
  149.2 0.3 fusion.19
  149.5 0.7 pad_maximum_fusion.1
  (52 shorter events, 0.4 us)
Async XLA Ops:
  0.6 12.2 %copy-start = (f32[128,32,128]{2,1,0:T(8,128)S(1)}, f32[128,32,128]{2,1,0:T(8,128)}, u32[]{:S(2)}) copy-start(f32[128,32,128]{2,1,0:T(8,128)} %param.9) | copy-start | bytes 6291460
  4.9 15.7 %collective-permute-start.5 = (f32[128,128]{1,0:T(8,128)}, f32[128,128]{1,0:T(8,128)S(1)}, u32[]{:S(2)}, u32[]{:S(2)}) collective-permute-start(f32[128,128]{1,0:T(8,128)} %get-tuple-element.14), channel_id=1, source_target_pairs={{0,8},{8,16},{16,24},{24,0},{1,9},{9,17},{17,25},{25,1},{2,10},{10... | collective-permute-start | bytes 196616 | tf_op jit(solution)/shard_map/ppermute | solution.py:13
  7.9 12.8 %collective-permute-start.6 = (f32[128,128]{1,0:T(8,128)}, f32[128,128]{1,0:T(8,128)S(1)}, u32[]{:S(2)}, u32[]{:S(2)}) collective-permute-start(f32[128,128]{1,0:T(8,128)} %get-tuple-element.15), channel_id=1, source_target_pairs={{0,24},{8,0},{16,8},{24,16},{1,25},{9,1},{17,9},{25,17},{2,26},{10... | collective-permute-start | bytes 196616 | tf_op jit(solution)/shard_map/ppermute | solution.py:13
  8.8 11.8 %collective-permute-start.7 = (f32[128,32]{1,0:T(8,128)}, f32[128,32]{1,0:T(8,128)S(1)}, u32[]{:S(2)}, u32[]{:S(2)}) collective-permute-start(f32[128,32]{1,0:T(8,128)} %get-tuple-element.16), channel_id=1, source_target_pairs={{0,1},{1,2},{2,3},{3,4},{4,5},{5,6},{6,7},{7,0},{8,9},{9,10},{10,1... | collective-permute-start | bytes 49160 | tf_op jit(solution)/shard_map/ppermute | solution.py:13
  8.8 11.8 %collective-permute-start.8 = (f32[128,32]{1,0:T(8,128)}, f32[128,32]{1,0:T(8,128)S(1)}, u32[]{:S(2)}, u32[]{:S(2)}) collective-permute-start(f32[128,32]{1,0:T(8,128)} %get-tuple-element.17), channel_id=1, source_target_pairs={{0,7},{1,0},{2,1},{3,2},{4,3},{5,4},{6,5},{7,6},{8,15},{9,8},{10,9... | collective-permute-start | bytes 49160 | tf_op jit(solution)/shard_map/ppermute | solution.py:13
  12.8 1.7 %copy-start.2 = (f32[128,32,128]{2,1,0:T(8,128)S(1)}, f32[128,32,128]{2,1,0:T(8,128)}, u32[]{:S(2)}) copy-start(f32[128,32,128]{2,1,0:T(8,128)} %param.8) | copy-start | bytes 6291460
  14.5 1.7 %copy-start.3 = (f32[16,8,32,128]{3,1,2,0:T(8,128)}, f32[16,8,32,128]{3,1,2,0:T(8,128)S(1)}, u32[]{:S(2)}) copy-start(f32[16,8,32,128]{3,1,2,0:T(8,128)S(1)} %copy.22) | copy-start | bytes 6291460
  16.2 3.5 %copy-start.4 = (f32[16,8,32,128]{3,1,2,0:T(8,128)}, f32[16,8,32,128]{3,1,2,0:T(8,128)S(1)}, u32[]{:S(2)}) copy-start(f32[16,8,32,128]{3,1,2,0:T(8,128)S(1)} %copy.23) | copy-start | bytes 6291460
  16.2 3.5 %copy-start.13 = (f32[128,128]{1,0:T(8,128)S(1)}, f32[128,128]{1,0:T(8,128)}, u32[]{:S(2)}) copy-start(f32[128,128]{1,0:T(8,128)} %param.12) | copy-start | bytes 196612
  16.2 3.6 %copy-start.14 = (f32[128,128]{1,0:T(8,128)S(1)}, f32[128,128]{1,0:T(8,128)}, u32[]{:S(2)}) copy-start(f32[128,128]{1,0:T(8,128)} %param.11) | copy-start | bytes 196612
  19.6 32.9 %collective-permute-start = (f32[128,256]{0,1:T(8,128)S(1)}, f32[128,256]{0,1:T(8,128)S(1)}, u32[]{:S(2)}, u32[]{:S(2)}) collective-permute-start(f32[128,256]{0,1:T(8,128)S(1)} %fusion.10), channel_id=1, source_target_pairs={{0,1},{1,0},{2,3},{3,2},{4,5},{5,4},{6,7},{7,6},{8,9},{9,8},{10,11... | collective-permute-start | bytes 393224 | tf_op jit(solution)/shard_map/ppermute | solution.py:107
  20.6 0.6 copy-start.7
  20.6 0.7 copy-start.8
  20.6 0.7 copy-start.5
  20.7 0.7 copy-start.6
  31.4 8.7 %collective-permute-start.9 = (f32[128,128]{1,0:T(8,128)}, f32[128,128]{1,0:T(8,128)S(1)}, u32[]{:S(2)}, u32[]{:S(2)}) collective-permute-start(f32[128,128]{1,0:T(8,128)} %get-tuple-element.19), channel_id=1, source_target_pairs={{0,8},{8,16},{16,24},{24,0},{1,9},{9,17},{17,25},{25,1},{2,10},{10... | collective-permute-start | bytes 196616 | tf_op jit(solution)/shard_map/ppermute | solution.py:13
  32.5 7.7 %collective-permute-start.10 = (f32[128,128]{1,0:T(8,128)}, f32[128,128]{1,0:T(8,128)S(1)}, u32[]{:S(2)}, u32[]{:S(2)}) collective-permute-start(f32[128,128]{1,0:T(8,128)} %get-tuple-element.20), channel_id=1, source_target_pairs={{0,24},{8,0},{16,8},{24,16},{1,25},{9,1},{17,9},{25,17},{2,26},{10... | collective-permute-start | bytes 196616 | tf_op jit(solution)/shard_map/ppermute | solution.py:13
  34.3 5.8 %collective-permute-start.11 = (f32[128,32]{1,0:T(8,128)}, f32[128,32]{1,0:T(8,128)S(1)}, u32[]{:S(2)}, u32[]{:S(2)}) collective-permute-start(f32[128,32]{1,0:T(8,128)} %get-tuple-element.21), channel_id=1, source_target_pairs={{0,1},{1,2},{2,3},{3,4},{4,5},{5,6},{6,7},{7,0},{8,9},{9,10},{10,1... | collective-permute-start | bytes 49160 | tf_op jit(solution)/shard_map/ppermute | solution.py:13
  34.3 5.8 %collective-permute-start.12 = (f32[128,32]{1,0:T(8,128)}, f32[128,32]{1,0:T(8,128)S(1)}, u32[]{:S(2)}, u32[]{:S(2)}) collective-permute-start(f32[128,32]{1,0:T(8,128)} %get-tuple-element.22), channel_id=1, source_target_pairs={{0,7},{1,0},{2,1},{3,2},{4,3},{5,4},{6,5},{7,6},{8,15},{9,8},{10,9... | collective-permute-start | bytes 49160 | tf_op jit(solution)/shard_map/ppermute | solution.py:13
  40.1 0.6 copy-start.11
  40.1 0.7 copy-start.12
  40.2 0.7 copy-start.9
  40.2 0.7 copy-start.10
  52.5 8.6 %copy-start.1 = (f32[128,4096]{1,0:T(8,128)}, f32[128,4096]{1,0:T(8,128)S(1)}, u32[]{:S(2)}) copy-start(f32[128,4096]{1,0:T(8,128)S(1)} %reshape.34) | copy-start | bytes 6291460
  52.6 8.7 %collective-permute-start.1 = (f32[128,256]{0,1:T(8,128)S(1)}, f32[128,256]{0,1:T(8,128)S(1)}, u32[]{:S(2)}, u32[]{:S(2)}) collective-permute-start(f32[128,256]{0,1:T(8,128)S(1)} %add.39), channel_id=1, source_target_pairs={{0,2},{1,3},{2,0},{3,1},{4,6},{5,7},{6,4},{7,5},{8,10},{9,11},{10,... | collective-permute-start | bytes 393224 | tf_op jit(solution)/shard_map/ppermute | solution.py:107
  61.2 10.7 %collective-permute-start.13 = (f32[128,384]{0,1:T(8,128)S(1)}, f32[128,384]{0,1:T(8,128)S(1)}, u32[]{:S(2)}, u32[]{:S(2)}) collective-permute-start(f32[128,384]{0,1:T(8,128)S(1)} %fusion), channel_id=1, source_target_pairs={{0,1},{1,0},{2,3},{3,2},{4,5},{5,4},{6,7},{7,6},{8,9},{9,8},{10,11... | collective-permute-start | bytes 589832 | tf_op jit(solution)/shard_map/ppermute | solution.py:107
  61.3 10.0 %collective-permute-start.2 = (f32[128,256]{0,1:T(8,128)S(1)}, f32[128,256]{0,1:T(8,128)S(1)}, u32[]{:S(2)}, u32[]{:S(2)}) collective-permute-start(f32[128,256]{0,1:T(8,128)S(1)} %add.40), channel_id=1, source_target_pairs={{0,4},{1,5},{2,6},{3,7},{4,0},{5,1},{6,2},{7,3},{8,12},{9,13},{10,... | collective-permute-start | bytes 393224 | tf_op jit(solution)/shard_map/ppermute | solution.py:107
  71.3 5.0 %collective-permute-start.3 = (f32[128,256]{0,1:T(8,128)S(1)}, f32[128,256]{0,1:T(8,128)S(1)}, u32[]{:S(2)}, u32[]{:S(2)}) collective-permute-start(f32[128,256]{0,1:T(8,128)S(1)} %add.41), channel_id=1, source_target_pairs={{0,8},{8,0},{16,24},{24,16},{1,9},{9,1},{17,25},{25,17},{2,10},{10... | collective-permute-start | bytes 393224 | tf_op jit(solution)/shard_map/ppermute | solution.py:107
  71.9 6.5 %collective-permute-start.14 = (f32[128,384]{0,1:T(8,128)S(1)}, f32[128,384]{0,1:T(8,128)S(1)}, u32[]{:S(2)}, u32[]{:S(2)}) collective-permute-start(f32[128,384]{0,1:T(8,128)S(1)} %add.44), channel_id=1, source_target_pairs={{0,2},{1,3},{2,0},{3,1},{4,6},{5,7},{6,4},{7,5},{8,10},{9,11},{10,... | collective-permute-start | bytes 589832 | tf_op jit(solution)/shard_map/ppermute | solution.py:107
  76.3 5.0 %collective-permute-start.4 = (f32[128,256]{0,1:T(8,128)S(1)}, f32[128,256]{0,1:T(8,128)S(1)}, u32[]{:S(2)}, u32[]{:S(2)}) collective-permute-start(f32[128,256]{0,1:T(8,128)S(1)} %add.42), channel_id=1, source_target_pairs={{0,16},{8,24},{16,0},{24,8},{1,17},{9,25},{17,1},{25,9},{2,18},{10... | collective-permute-start | bytes 393224 | tf_op jit(solution)/shard_map/ppermute | solution.py:107
  78.4 26.3 %collective-permute-start.15 = (f32[128,384]{0,1:T(8,128)S(1)}, f32[128,384]{0,1:T(8,128)S(1)}, u32[]{:S(2)}, u32[]{:S(2)}) collective-permute-start(f32[128,384]{0,1:T(8,128)S(1)} %add.45), channel_id=1, source_target_pairs={{0,4},{1,5},{2,6},{3,7},{4,0},{5,1},{6,2},{7,3},{8,12},{9,13},{10,... | collective-permute-start | bytes 589832 | tf_op jit(solution)/shard_map/ppermute | solution.py:107
  104.7 5.7 %collective-permute-start.16 = (f32[128,384]{0,1:T(8,128)S(1)}, f32[128,384]{0,1:T(8,128)S(1)}, u32[]{:S(2)}, u32[]{:S(2)}) collective-permute-start(f32[128,384]{0,1:T(8,128)S(1)} %add.46), channel_id=1, source_target_pairs={{0,8},{8,0},{16,24},{24,16},{1,9},{9,1},{17,25},{25,17},{2,10},{10... | collective-permute-start | bytes 589832 | tf_op jit(solution)/shard_map/ppermute | solution.py:107
  110.5 5.7 %collective-permute-start.17 = (f32[128,384]{0,1:T(8,128)S(1)}, f32[128,384]{0,1:T(8,128)S(1)}, u32[]{:S(2)}, u32[]{:S(2)}) collective-permute-start(f32[128,384]{0,1:T(8,128)S(1)} %add.47), channel_id=1, source_target_pairs={{0,16},{8,24},{16,0},{24,8},{1,17},{9,25},{17,1},{25,9},{2,18},{10... | collective-permute-start | bytes 589832 | tf_op jit(solution)/shard_map/ppermute | solution.py:107
where the time goes:
time: 153 us; the launch traced here: 151 us
  other arithmetic  47.9 us (31%)
  starting transfers between devices  25.1 us (16%)
  Pallas kernels  24.3 us (16%)
  matrix products  23.8 us (16%)
  waiting for transfers between devices  18.4 us (12%)
  local copies, waits for them, and re-layouts  9.53 us (6%)
  between operations  1.55 us (1%)
    another operation x6, other arithmetic, lower_inverse(): low = jnp.linalg.cholesky(matrix)  25 us
    dot_general x10, matrix products, hdot(): return jnp.dot(a, b, precision=lax.Precision.HIGHEST)  23.2 us
    another operation x4, other arithmetic, lower_inverse(): return jax.scipy.linalg.solve_triangular(low, identity, lower=True)  20.9 us
    pallas_call x2, Pallas kernels, substep_call(): pl.pallas_call(functools.partial(substep_kernel, count=count, rows=rows,...  20 us
    ppermute x10, waiting for transfers between devices, exchange_sum(): array = array + lax.ppermute(array, axis, pairs)  16.1 us
    ppermute x8, starting transfers between devices, neighbour(): return lax.ppermute(array, axis, pairs)  14.4 us
    ppermute x10, starting transfers between devices, exchange_sum(): array = array + lax.ppermute(array, axis, pairs)  10.7 us
    unnamed x35, local copies, waits for them, and re-layouts  7.6 us
  transfers between devices with their start and end apart: 18, of which 6 were waited for; matrix products, arithmetic and copies ran while one was open for 31% of the time, Pallas kernels for 13%

commit v1 on v0

--- a/solution.py
+++ b/solution.py
@@ -113,10 +113,42 @@
     return jnp.dot(a, b, precision=lax.Precision.HIGHEST)
 
 
+def inverse_kernel(a_ref, x_ref, *, size):
+    sub = lax.broadcasted_iota(jnp.int32, (size, size), 0)
+    lane = lax.broadcasted_iota(jnp.int32, (size, size), 1)
+    lane_row = lax.broadcasted_iota(jnp.int32, (1, size), 1)
+    sub_col = lax.broadcasted_iota(jnp.int32, (size, 1), 0)
+
+    def step(k, carry):
+        a, x = carry
+        row = jnp.sum(jnp.where(sub == k, a, 0.0), axis=0, keepdims=True)
+        col = jnp.sum(jnp.where(lane == k, a, 0.0), axis=1, keepdims=True)
+        pivot = jnp.sum(jnp.where(lane_row == k, row, 0.0), axis=1, keepdims=True)
+        root = jnp.sqrt(pivot)
+        low_row = jnp.where(lane_row >= k, row, 0.0) / root
+        low_col = jnp.where(sub_col >= k, col, 0.0) / root
+        x_row = jnp.sum(jnp.where(sub == k, x, 0.0), axis=0, keepdims=True) / root
+        a = a - low_col * low_row
+        x = jnp.where(sub == k, x_row, x - jnp.where(sub_col > k, low_col, 0.0) * x_row)
+        return a, x
+
+    eye = jnp.where(sub == lane, 1.0, 0.0).astype(jnp.float32)
+    _, x = lax.fori_loop(0, size, step, (a_ref[...], eye), unroll=4)
+    x_ref[...] = x
+
+
+def lower_inverse_call(matrix):
+    size = matrix.shape[0]
+    vmem = pl.BlockSpec(memory_space=pltpu.VMEM)
+    return pl.pallas_call(
+        functools.partial(inverse_kernel, size=size),
+        out_shape=jax.ShapeDtypeStruct((size, size), jnp.float32),
+        in_specs=[vmem],
+        out_specs=vmem,
+    )(matrix)
+
 def lower_inverse(matrix):
-    low = jnp.linalg.cholesky(matrix)
-    identity = jnp.eye(matrix.shape[0], dtype=matrix.dtype)
-    return jax.scipy.linalg.solve_triangular(low, identity, lower=True)
+    return lower_inverse_call(0.5 * (matrix + matrix.T))
 
 
 def body(basis_fields, carried_fields, velocity, diffusion, advection):

time: 153 us -> 145 us (0.948)
  other arithmetic: 47.9 us -> 3.24 us
  Pallas kernels: 24.3 us -> 61.6 us
    another operation x10 -> x0, other arithmetic: 45.9 us -> none  [the longest x6 25 us: lower_inverse(): low = jnp.linalg.cholesky(matrix)]
    pallas_call x0 -> x2, Pallas kernels: none -> 37.3 us  [lower_inverse_call(): pl.pallas_call(functools.partial(inverse_kernel, size=size), out_shape=ja...]
    unnamed x35 -> x39, local copies, waits for them, and re-layouts: 7.6 us -> 7.59 us
  transfers between devices with their start and end apart: 18 -> 18, of which waited for: 6 -> 6; matrix products, arithmetic and copies ran while one was open for 31% -> 16% of each run, Pallas kernels for 13% -> 27%
where the time goes in v1:
time: 145 us; the launch traced here: 142 us
  Pallas kernels  61.6 us (42%)
  starting transfers between devices  25.2 us (17%)
  matrix products  23.1 us (16%)
  waiting for transfers between devices  18.3 us (13%)
  local copies, waits for them, and re-layouts  9.72 us (7%)
  other arithmetic  3.24 us (2%)
    pallas_call x2, Pallas kernels, lower_inverse_call(): pl.pallas_call(functools.partial(inverse_kernel, size=size), out_shape=ja...  37.3 us
    dot_general x10, matrix products, hdot(): return jnp.dot(a, b, precision=lax.Precision.HIGHEST)  23.1 us
    pallas_call x2, Pallas kernels, substep_call(): pl.pallas_call(functools.partial(substep_kernel, count=count, rows=rows,...  20 us
    ppermute x10, waiting for transfers between devices, exchange_sum(): array = array + lax.ppermute(array, axis, pairs)  16 us
    ppermute x8, starting transfers between devices, neighbour(): return lax.ppermute(array, axis, pairs)  14.4 us
    ppermute x10, starting transfers between devices, exchange_sum(): array = array + lax.ppermute(array, axis, pairs)  10.8 us
    unnamed x39, local copies, waits for them, and re-layouts  7.59 us
    pallas_call x1, Pallas kernels, edges_call(): pl.pallas_call(functools.partial(edges_kernel, count=count, rows=rows, co...  4.3 us
  transfers between devices with their start and end apart: 18, of which 6 were waited for; matrix products, arithmetic and copies ran while one was open for 16% of the time, Pallas kernels for 27%

profile of v1, /device:TPU:0, one launch (start us, length us, event | category | flops | bytes accessed | tf_op | source)
XLA Modules:
  0.0 142.5 jit_solution(14188175230297165408)
XLA Ops:
  0.6 0.0 copy-start
  0.6 4.3 %shard_map.69 = (f32[128,128]{1,0:T(8,128)}, f32[128,128]{1,0:T(8,128)}, f32[128,32]{1,0:T(8,128)}, f32[128,32]{1,0:T(8,128)}) custom-call(f32[4096,128]{1,0:T(8,128)} %bitcast.41), custom_call_target="tpu_custom_call" | custom-call | tf_op jit(solution)/shard_map/pallas_call | solution.py:73
  4.9 2.9 %collective-permute-start.5 = (f32[128,128]{1,0:T(8,128)}, f32[128,128]{1,0:T(8,128)S(1)}, u32[]{:S(2)}, u32[]{:S(2)}) collective-permute-start(f32[128,128]{1,0:T(8,128)} %get-tuple-element.12), channel_id=1, source_target_pairs={{0,8},{8,16},{16,24},{24,0},{1,9},{9,17},{17,25},{25,1},{2,10},{10... | collective-permute-start | bytes 196616 | tf_op jit(solution)/shard_map/ppermute | solution.py:13
  7.9 1.0 collective-permute-start.6
  8.8 4.0 %collective-permute-start.8 = (f32[128,32]{1,0:T(8,128)}, f32[128,32]{1,0:T(8,128)S(1)}, u32[]{:S(2)}, u32[]{:S(2)}) collective-permute-start(f32[128,32]{1,0:T(8,128)} %get-tuple-element.15), channel_id=1, source_target_pairs={{0,7},{1,0},{2,1},{3,2},{4,3},{5,4},{6,5},{7,6},{8,15},{9,8},{10,9... | collective-permute-start | bytes 49160 | tf_op jit(solution)/shard_map/ppermute | solution.py:13
  12.9 1.7 %copy.22 = f32[16,8,32,128]{3,1,2,0:T(8,128)S(1)} copy(f32[16,8,32,128]{3,2,1,0:T(8,128)S(1)} %bitcast.43) | data formatting | bytes 4194304
  14.6 1.6 %copy.23 = f32[16,8,32,128]{3,1,2,0:T(8,128)S(1)} copy(f32[16,8,32,128]{3,2,1,0:T(8,128)S(1)} %bitcast.45) | data formatting | bytes 4194304
  16.2 0.0 copy-start.15
  16.3 0.0 copy-start.16
  16.3 3.4 %fusion.10 = f32[128,256]{0,1:T(8,128)S(1)} fusion(f32[128,4096]{1,0:T(8,128)S(1)} %bitcast.48, f32[128,4096]{1,0:T(8,128)S(1)} %bitcast.46), kind=kOutput, calls=%fused_computation.14 | convolution fusion | flops 1611661312 | bytes 4325376 | tf_op jit(solution)/shard_map/dot_general | solution.py:113
  19.7 0.1 collective-permute-start
  19.8 0.1 copy.9
  19.9 0.1 copy.8
  20.0 0.7 pad_maximum_fusion.mix_ref
  20.7 0.0 collective-permute-done.5.above_ref
  20.7 0.6 copy-done.9
  21.3 0.0 copy-done.10
  21.3 0.0 copy-done.7
  21.4 0.0 copy-done.8
  21.4 10.1 %shard_map.70 = (f32[4096,128]{1,0:T(8,128)}, f32[128,128]{1,0:T(8,128)}, f32[128,128]{1,0:T(8,128)}, f32[128,32]{1,0:T(8,128)}, f32[128,32]{1,0:T(8,128)}) custom-call(f32[4096,128]{1,0:T(8,128)} %bitcast.42, f32[128,128]{1,0:T(8,128)} %copy-done.7, f32[128,128]{1,0:T(8,128)} %copy-done.8, f32[128,32]{1,0:T(8,128)} %copy-done.9, f32[128,32]{1,0:T(8,128)} %copy-done.10, ...), custom_call_target="tpu_custom_call" | custom-call | tf_op jit(solution)/shard_map/pallas_call | solution.py:83
  31.4 1.1 collective-permute-start.9
  32.5 1.9 %collective-permute-start.10 = (f32[128,128]{1,0:T(8,128)}, f32[128,128]{1,0:T(8,128)S(1)}, u32[]{:S(2)}, u32[]{:S(2)}) collective-permute-start(f32[128,128]{1,0:T(8,128)} %get-tuple-element.18), channel_id=1, source_target_pairs={{0,24},{8,0},{16,8},{24,16},{1,25},{9,1},{17,9},{25,17},{2,26},{10... | collective-permute-start | bytes 196616 | tf_op jit(solution)/shard_map/ppermute | solution.py:13
  34.4 0.0 collective-permute-start.11
  34.4 3.5 %collective-permute-start.12 = (f32[128,32]{1,0:T(8,128)}, f32[128,32]{1,0:T(8,128)S(1)}, u32[]{:S(2)}, u32[]{:S(2)}) collective-permute-start(f32[128,32]{1,0:T(8,128)} %get-tuple-element.20), channel_id=1, source_target_pairs={{0,7},{1,0},{2,1},{3,2},{4,3},{5,4},{6,5},{7,6},{8,15},{9,8},{10,9... | collective-permute-start | bytes 49160 | tf_op jit(solution)/shard_map/ppermute | solution.py:13
  37.9 2.3 %collective-permute-done.11.left_ref = f32[128,32]{1,0:T(8,128)S(1)} collective-permute-done((f32[128,32]{1,0:T(8,128)}, f32[128,32]{1,0:T(8,128)S(1)}, u32[]{:S(2)}, u32[]{:S(2)}) %collective-permute-start.11) | collective-permute-done | bytes 16416 | tf_op jit(solution)/shard_map/ppermute | solution.py:13
  40.2 0.0 collective-permute-done.9.above_ref
  40.2 0.6 copy-done.13
  40.8 0.0 copy-done.14
  40.8 0.0 copy-done.11
  40.9 10.0 %shard_map.71 = (f32[4096,128]{1,0:T(8,128)}, f32[128,128]{1,0:T(8,128)}, f32[128,128]{1,0:T(8,128)}, f32[128,32]{1,0:T(8,128)}, f32[128,32]{1,0:T(8,128)}) custom-call(f32[4096,128]{1,0:T(8,128)} %get-tuple-element.16.f_ref, f32[128,128]{1,0:T(8,128)} %copy-done.11, f32[128,128]{1,0:T(8,128)} %copy-done.12, f32[128,32]{1,0:T(8,128)} %copy-done.13, ...), custom_call_target="tpu_custom_call" | custom-call | tf_op jit(solution)/shard_map/pallas_call | solution.py:83
  50.8 1.9 %reshape.26 = f32[128,4096]{1,0:T(8,128)S(1)} reshape(f32[4096,128]{1,0:T(8,128)} %get-tuple-element.21) | data formatting | bytes 4194304 | tf_op jit(solution)/shard_map/reshape | solution.py:171
  52.8 0.0 copy-start.1
  52.8 0.1 collective-permute-start.1
  52.9 8.3 %fusion = f32[128,384]{0,1:T(8,128)S(1)} fusion(f32[128,4096]{1,0:T(8,128)S(1)} %reshape.26, f32[128,4096]{1,0:T(8,128)} %bitcast.47, f32[128,4096]{1,0:T(8,128)} %bitcast.49), kind=kOutput, calls=%fused_computation | convolution fusion | flops 2419064832 | bytes 6488064 | tf_op jit(solution)/shard_map/dot_general | solution.py:113
  61.2 0.1 collective-permute-start.13
  61.3 3.5 %collective-permute-start.2 = (f32[128,256]{0,1:T(8,128)S(1)}, f32[128,256]{0,1:T(8,128)S(1)}, u32[]{:S(2)}, u32[]{:S(2)}) collective-permute-start(f32[128,256]{0,1:T(8,128)S(1)} %add.37), channel_id=1, source_target_pairs={{0,4},{1,5},{2,6},{3,7},{4,0},{5,1},{6,2},{7,3},{8,12},{9,13},{10,... | collective-permute-start | bytes 393224 | tf_op jit(solution)/shard_map/ppermute | solution.py:107
  64.8 6.5 %collective-permute-done.2 = f32[128,256]{0,1:T(8,128)S(1)} collective-permute-done((f32[128,256]{0,1:T(8,128)S(1)}, f32[128,256]{0,1:T(8,128)S(1)}, u32[]{:S(2)}, u32[]{:S(2)}) %collective-permute-start.2) | collective-permute-done | bytes 131104 | tf_op jit(solution)/shard_map/ppermute | solution.py:107
  71.3 0.6 collective-permute-start.3
  71.9 0.3 collective-permute-start.14
  72.2 4.1 %collective-permute-done.3 = f32[128,256]{0,1:T(8,128)S(1)} collective-permute-done((f32[128,256]{0,1:T(8,128)S(1)}, f32[128,256]{0,1:T(8,128)S(1)}, u32[]{:S(2)}, u32[]{:S(2)}) %collective-permute-start.3) | collective-permute-done | bytes 131104 | tf_op jit(solution)/shard_map/ppermute | solution.py:107
  76.3 2.1 %collective-permute-start.4 = (f32[128,256]{0,1:T(8,128)S(1)}, f32[128,256]{0,1:T(8,128)S(1)}, u32[]{:S(2)}, u32[]{:S(2)}) collective-permute-start(f32[128,256]{0,1:T(8,128)S(1)} %add.39), channel_id=1, source_target_pairs={{0,16},{8,24},{16,0},{24,8},{1,17},{9,25},{17,1},{25,9},{2,18},{10... | collective-permute-start | bytes 393224 | tf_op jit(solution)/shard_map/ppermute | solution.py:107
  78.4 1.5 %collective-permute-start.15 = (f32[128,384]{0,1:T(8,128)S(1)}, f32[128,384]{0,1:T(8,128)S(1)}, u32[]{:S(2)}, u32[]{:S(2)}) collective-permute-start(f32[128,384]{0,1:T(8,128)S(1)} %add.43), channel_id=1, source_target_pairs={{0,4},{1,5},{2,6},{3,7},{4,0},{5,1},{6,2},{7,3},{8,12},{9,13},{10,... | collective-permute-start | bytes 589832 | tf_op jit(solution)/shard_map/ppermute | solution.py:107
  79.9 1.4 %collective-permute-done.4 = f32[128,256]{0,1:T(8,128)S(1)} collective-permute-done((f32[128,256]{0,1:T(8,128)S(1)}, f32[128,256]{0,1:T(8,128)S(1)}, u32[]{:S(2)}, u32[]{:S(2)}) %collective-permute-start.4) | collective-permute-done | bytes 131104 | tf_op jit(solution)/shard_map/ppermute | solution.py:107
  81.4 0.1 copy.7
  81.5 0.6 fusion.19.a_ref
  82.2 18.6 %shard_map.68 = f32[128,128]{1,0:T(8,128)} custom-call(f32[128,128]{1,0:T(8,128)} %fusion.19.a_ref), custom_call_target="tpu_custom_call" | custom-call | tf_op jit(solution)/shard_map/pallas_call | solution.py:143
  100.8 0.6 collective-permute-start.16
  101.4 4.6 %fusion.22 = f32[128,4096]{1,0:T(8,128)S(1)} fusion(f32[128,128]{1,0:T(8,128)} %shard_map.68, f32[16,8,32,128]{3,2,1,0:T(8,128)} %bitcast.44), kind=kOutput, calls=%fused_computation.33 | convolution fusion | flops 805306368 | bytes 4259840 | tf_op jit(solution)/shard_map/dot_general | solution.py:113
  106.0 0.5 collective-permute-done.16
  106.6 2.1 %collective-permute-start.17 = (f32[128,384]{0,1:T(8,128)S(1)}, f32[128,384]{0,1:T(8,128)S(1)}, u32[]{:S(2)}, u32[]{:S(2)}) collective-permute-start(f32[128,384]{0,1:T(8,128)S(1)} %add.45), channel_id=1, source_target_pairs={{0,16},{8,24},{16,0},{24,8},{1,17},{9,25},{17,1},{25,9},{2,18},{10... | collective-permute-start | bytes 589832 | tf_op jit(solution)/shard_map/ppermute | solution.py:107
  108.7 0.3 fusion.14
  108.9 3.4 %collective-permute-done.17 = f32[128,384]{0,1:T(8,128)S(1)} collective-permute-done((f32[128,384]{0,1:T(8,128)S(1)}, f32[128,384]{0,1:T(8,128)S(1)}, u32[]{:S(2)}, u32[]{:S(2)}) %collective-permute-start.17) | collective-permute-done | bytes 196640 | tf_op jit(solution)/shard_map/ppermute | solution.py:107
  112.4 0.3 fusion.16
  112.7 0.3 slice_subtract_fusion.2
  112.9 0.1 copy.13
  113.0 0.6 fusion.18.a_ref
  113.7 18.6 %shard_map.72 = f32[128,128]{1,0:T(8,128)} custom-call(f32[128,128]{1,0:T(8,128)} %fusion.18.a_ref), custom_call_target="tpu_custom_call" | custom-call | tf_op jit(solution)/shard_map/pallas_call | solution.py:143
  132.3 3.6 %convolution_subtract_fusion = f32[128,4096]{1,0:T(8,128)S(1)} fusion(f32[128,4096]{1,0:T(8,128)} %copy-done.1, f32[128,128]{1,0:T(8,128)S(1)} %fusion.16, f32[128,4096]{1,0:T(8,128)S(1)} %fusion.22), kind=kOutput, calls=%fused_computation.6 | convolution fusion | flops 805830656 | bytes 6356992 | tf_op jit(solution)/shard_map/dot_general | solution.py:113
  135.9 1.9 %fusion.23 = f32[128,4096]{1,0:T(8,128)S(1)} fusion(f32[128,128]{1,0:T(8,128)S(1)} %copy-done.6, f32[128,4096]{1,0:T(8,128)S(1)} %convolution_subtract_fusion), kind=kOutput, calls=%fused_computation.34 | convolution fusion | flops 805306368 | bytes 4259840 | tf_op jit(solution)/shard_map/dot_general | solution.py:113
  137.8 0.4 maximum_bitcast_fusion
  138.2 2.8 %copy.18 = f32[32,8,32,128]{3,2,1,0:T(8,128)} copy(f32[32,8,32,128]{3,1,2,0:T(8,128)S(1)} %maximum_bitcast_fusion) | data formatting | bytes 8388608
  141.0 0.3 fusion.24
  141.3 0.3 fusion.13
  141.5 0.7 pad_maximum_fusion.1
  (46 shorter events, 0.3 us)
Async XLA Ops:
  0.6 12.3 %copy-start = (f32[128,32,128]{2,1,0:T(8,128)S(1)}, f32[128,32,128]{2,1,0:T(8,128)}, u32[]{:S(2)}) copy-start(f32[128,32,128]{2,1,0:T(8,128)} %param.6) | copy-start | bytes 6291460
  4.9 15.7 %collective-permute-start.5 = (f32[128,128]{1,0:T(8,128)}, f32[128,128]{1,0:T(8,128)S(1)}, u32[]{:S(2)}, u32[]{:S(2)}) collective-permute-start(f32[128,128]{1,0:T(8,128)} %get-tuple-element.12), channel_id=1, source_target_pairs={{0,8},{8,16},{16,24},{24,0},{1,9},{9,17},{17,25},{25,1},{2,10},{10... | collective-permute-start | bytes 196616 | tf_op jit(solution)/shard_map/ppermute | solution.py:13
  7.9 12.8 %collective-permute-start.6 = (f32[128,128]{1,0:T(8,128)}, f32[128,128]{1,0:T(8,128)S(1)}, u32[]{:S(2)}, u32[]{:S(2)}) collective-permute-start(f32[128,128]{1,0:T(8,128)} %get-tuple-element.13), channel_id=1, source_target_pairs={{0,24},{8,0},{16,8},{24,16},{1,25},{9,1},{17,9},{25,17},{2,26},{10... | collective-permute-start | bytes 196616 | tf_op jit(solution)/shard_map/ppermute | solution.py:13
  8.8 11.8 %collective-permute-start.7 = (f32[128,32]{1,0:T(8,128)}, f32[128,32]{1,0:T(8,128)S(1)}, u32[]{:S(2)}, u32[]{:S(2)}) collective-permute-start(f32[128,32]{1,0:T(8,128)} %get-tuple-element.14), channel_id=1, source_target_pairs={{0,1},{1,2},{2,3},{3,4},{4,5},{5,6},{6,7},{7,0},{8,9},{9,10},{10,1... | collective-permute-start | bytes 49160 | tf_op jit(solution)/shard_map/ppermute | solution.py:13
  8.8 11.8 %collective-permute-start.8 = (f32[128,32]{1,0:T(8,128)}, f32[128,32]{1,0:T(8,128)S(1)}, u32[]{:S(2)}, u32[]{:S(2)}) collective-permute-start(f32[128,32]{1,0:T(8,128)} %get-tuple-element.15), channel_id=1, source_target_pairs={{0,7},{1,0},{2,1},{3,2},{4,3},{5,4},{6,5},{7,6},{8,15},{9,8},{10,9... | collective-permute-start | bytes 49160 | tf_op jit(solution)/shard_map/ppermute | solution.py:13
  12.9 1.7 %copy-start.2 = (f32[128,32,128]{2,1,0:T(8,128)S(1)}, f32[128,32,128]{2,1,0:T(8,128)}, u32[]{:S(2)}) copy-start(f32[128,32,128]{2,1,0:T(8,128)} %param.5) | copy-start | bytes 6291460
  14.6 1.7 %copy-start.3 = (f32[16,8,32,128]{3,1,2,0:T(8,128)}, f32[16,8,32,128]{3,1,2,0:T(8,128)S(1)}, u32[]{:S(2)}) copy-start(f32[16,8,32,128]{3,1,2,0:T(8,128)S(1)} %copy.22) | copy-start | bytes 6291460
  16.2 3.5 %copy-start.4 = (f32[16,8,32,128]{3,1,2,0:T(8,128)}, f32[16,8,32,128]{3,1,2,0:T(8,128)S(1)}, u32[]{:S(2)}) copy-start(f32[16,8,32,128]{3,1,2,0:T(8,128)S(1)} %copy.23) | copy-start | bytes 6291460
  16.2 3.5 %copy-start.15 = (f32[128,128]{1,0:T(8,128)S(1)}, f32[128,128]{1,0:T(8,128)}, u32[]{:S(2)}) copy-start(f32[128,128]{1,0:T(8,128)} %param.9) | copy-start | bytes 196612
  16.3 3.6 %copy-start.16 = (f32[128,128]{1,0:T(8,128)S(1)}, f32[128,128]{1,0:T(8,128)}, u32[]{:S(2)}) copy-start(f32[128,128]{1,0:T(8,128)} %param.8) | copy-start | bytes 196612
  19.7 33.1 %collective-permute-start = (f32[128,256]{0,1:T(8,128)S(1)}, f32[128,256]{0,1:T(8,128)S(1)}, u32[]{:S(2)}, u32[]{:S(2)}) collective-permute-start(f32[128,256]{0,1:T(8,128)S(1)} %fusion.10), channel_id=1, source_target_pairs={{0,1},{1,0},{2,3},{3,2},{4,5},{5,4},{6,7},{7,6},{8,9},{9,8},{10,11... | collective-permute-start | bytes 393224 | tf_op jit(solution)/shard_map/ppermute | solution.py:107
  20.7 0.6 copy-start.9
  20.7 0.6 copy-start.10
  20.7 0.7 copy-start.7
  20.7 0.7 copy-start.8
  31.4 8.7 %collective-permute-start.9 = (f32[128,128]{1,0:T(8,128)}, f32[128,128]{1,0:T(8,128)S(1)}, u32[]{:S(2)}, u32[]{:S(2)}) collective-permute-start(f32[128,128]{1,0:T(8,128)} %get-tuple-element.17), channel_id=1, source_target_pairs={{0,8},{8,16},{16,24},{24,0},{1,9},{9,17},{17,25},{25,1},{2,10},{10... | collective-permute-start | bytes 196616 | tf_op jit(solution)/shard_map/ppermute | solution.py:13
  32.5 7.7 %collective-permute-start.10 = (f32[128,128]{1,0:T(8,128)}, f32[128,128]{1,0:T(8,128)S(1)}, u32[]{:S(2)}, u32[]{:S(2)}) collective-permute-start(f32[128,128]{1,0:T(8,128)} %get-tuple-element.18), channel_id=1, source_target_pairs={{0,24},{8,0},{16,8},{24,16},{1,25},{9,1},{17,9},{25,17},{2,26},{10... | collective-permute-start | bytes 196616 | tf_op jit(solution)/shard_map/ppermute | solution.py:13
  34.4 5.8 %collective-permute-start.11 = (f32[128,32]{1,0:T(8,128)}, f32[128,32]{1,0:T(8,128)S(1)}, u32[]{:S(2)}, u32[]{:S(2)}) collective-permute-start(f32[128,32]{1,0:T(8,128)} %get-tuple-element.19), channel_id=1, source_target_pairs={{0,1},{1,2},{2,3},{3,4},{4,5},{5,6},{6,7},{7,0},{8,9},{9,10},{10,1... | collective-permute-start | bytes 49160 | tf_op jit(solution)/shard_map/ppermute | solution.py:13
  34.4 5.8 %collective-permute-start.12 = (f32[128,32]{1,0:T(8,128)}, f32[128,32]{1,0:T(8,128)S(1)}, u32[]{:S(2)}, u32[]{:S(2)}) collective-permute-start(f32[128,32]{1,0:T(8,128)} %get-tuple-element.20), channel_id=1, source_target_pairs={{0,7},{1,0},{2,1},{3,2},{4,3},{5,4},{6,5},{7,6},{8,15},{9,8},{10,9... | collective-permute-start | bytes 49160 | tf_op jit(solution)/shard_map/ppermute | solution.py:13
  40.2 0.6 copy-start.13
  40.2 0.7 copy-start.14
  40.2 0.7 copy-start.11
  40.2 0.7 copy-start.12
  52.8 8.4 %copy-start.1 = (f32[128,4096]{1,0:T(8,128)}, f32[128,4096]{1,0:T(8,128)S(1)}, u32[]{:S(2)}) copy-start(f32[128,4096]{1,0:T(8,128)S(1)} %reshape.26) | copy-start | bytes 6291460
  52.8 8.4 %collective-permute-start.1 = (f32[128,256]{0,1:T(8,128)S(1)}, f32[128,256]{0,1:T(8,128)S(1)}, u32[]{:S(2)}, u32[]{:S(2)}) collective-permute-start(f32[128,256]{0,1:T(8,128)S(1)} %add.36), channel_id=1, source_target_pairs={{0,2},{1,3},{2,0},{3,1},{4,6},{5,7},{6,4},{7,5},{8,10},{9,11},{10,... | collective-permute-start | bytes 393224 | tf_op jit(solution)/shard_map/ppermute | solution.py:107
  61.2 10.7 %collective-permute-start.13 = (f32[128,384]{0,1:T(8,128)S(1)}, f32[128,384]{0,1:T(8,128)S(1)}, u32[]{:S(2)}, u32[]{:S(2)}) collective-permute-start(f32[128,384]{0,1:T(8,128)S(1)} %fusion), channel_id=1, source_target_pairs={{0,1},{1,0},{2,3},{3,2},{4,5},{5,4},{6,7},{7,6},{8,9},{9,8},{10,11... | collective-permute-start | bytes 589832 | tf_op jit(solution)/shard_map/ppermute | solution.py:107
  61.3 10.0 %collective-permute-start.2 = (f32[128,256]{0,1:T(8,128)S(1)}, f32[128,256]{0,1:T(8,128)S(1)}, u32[]{:S(2)}, u32[]{:S(2)}) collective-permute-start(f32[128,256]{0,1:T(8,128)S(1)} %add.37), channel_id=1, source_target_pairs={{0,4},{1,5},{2,6},{3,7},{4,0},{5,1},{6,2},{7,3},{8,12},{9,13},{10,... | collective-permute-start | bytes 393224 | tf_op jit(solution)/shard_map/ppermute | solution.py:107
  71.3 5.0 %collective-permute-start.3 = (f32[128,256]{0,1:T(8,128)S(1)}, f32[128,256]{0,1:T(8,128)S(1)}, u32[]{:S(2)}, u32[]{:S(2)}) collective-permute-start(f32[128,256]{0,1:T(8,128)S(1)} %add.38), channel_id=1, source_target_pairs={{0,8},{8,0},{16,24},{24,16},{1,9},{9,1},{17,25},{25,17},{2,10},{10... | collective-permute-start | bytes 393224 | tf_op jit(solution)/shard_map/ppermute | solution.py:107
  71.9 6.5 %collective-permute-start.14 = (f32[128,384]{0,1:T(8,128)S(1)}, f32[128,384]{0,1:T(8,128)S(1)}, u32[]{:S(2)}, u32[]{:S(2)}) collective-permute-start(f32[128,384]{0,1:T(8,128)S(1)} %add.42), channel_id=1, source_target_pairs={{0,2},{1,3},{2,0},{3,1},{4,6},{5,7},{6,4},{7,5},{8,10},{9,11},{10,... | collective-permute-start | bytes 589832 | tf_op jit(solution)/shard_map/ppermute | solution.py:107
  76.3 5.0 %collective-permute-start.4 = (f32[128,256]{0,1:T(8,128)S(1)}, f32[128,256]{0,1:T(8,128)S(1)}, u32[]{:S(2)}, u32[]{:S(2)}) collective-permute-start(f32[128,256]{0,1:T(8,128)S(1)} %add.39), channel_id=1, source_target_pairs={{0,16},{8,24},{16,0},{24,8},{1,17},{9,25},{17,1},{25,9},{2,18},{10... | collective-permute-start | bytes 393224 | tf_op jit(solution)/shard_map/ppermute | solution.py:107
  78.4 22.4 %collective-permute-start.15 = (f32[128,384]{0,1:T(8,128)S(1)}, f32[128,384]{0,1:T(8,128)S(1)}, u32[]{:S(2)}, u32[]{:S(2)}) collective-permute-start(f32[128,384]{0,1:T(8,128)S(1)} %add.43), channel_id=1, source_target_pairs={{0,4},{1,5},{2,6},{3,7},{4,0},{5,1},{6,2},{7,3},{8,12},{9,13},{10,... | collective-permute-start | bytes 589832 | tf_op jit(solution)/shard_map/ppermute | solution.py:107
  100.8 7.8 %copy-start.5 = (f32[128,128]{1,0:T(8,128)S(1)}, f32[128,128]{1,0:T(8,128)}, u32[]{:S(2)}) copy-start(f32[128,128]{1,0:T(8,128)} %shard_map.68) | copy-start | bytes 196612
  100.8 5.7 %collective-permute-start.16 = (f32[128,384]{0,1:T(8,128)S(1)}, f32[128,384]{0,1:T(8,128)S(1)}, u32[]{:S(2)}, u32[]{:S(2)}) collective-permute-start(f32[128,384]{0,1:T(8,128)S(1)} %add.44), channel_id=1, source_target_pairs={{0,8},{8,0},{16,24},{24,16},{1,9},{9,1},{17,25},{25,17},{2,10},{10... | collective-permute-start | bytes 589832 | tf_op jit(solution)/shard_map/ppermute | solution.py:107
  106.6 5.7 %collective-permute-start.17 = (f32[128,384]{0,1:T(8,128)S(1)}, f32[128,384]{0,1:T(8,128)S(1)}, u32[]{:S(2)}, u32[]{:S(2)}) collective-permute-start(f32[128,384]{0,1:T(8,128)S(1)} %add.45), channel_id=1, source_target_pairs={{0,16},{8,24},{16,0},{24,8},{1,17},{9,25},{17,1},{25,9},{2,18},{10... | collective-permute-start | bytes 589832 | tf_op jit(solution)/shard_map/ppermute | solution.py:107
  132.3 3.6 %copy-start.6 = (f32[128,128]{1,0:T(8,128)S(1)}, f32[128,128]{1,0:T(8,128)}, u32[]{:S(2)}) copy-start(f32[128,128]{1,0:T(8,128)} %shard_map.72) | copy-start | bytes 196612

commit v2 on v1

--- a/solution.py
+++ b/solution.py
@@ -124,10 +124,10 @@
         row = jnp.sum(jnp.where(sub == k, a, 0.0), axis=0, keepdims=True)
         col = jnp.sum(jnp.where(lane == k, a, 0.0), axis=1, keepdims=True)
         pivot = jnp.sum(jnp.where(lane_row == k, row, 0.0), axis=1, keepdims=True)
-        root = jnp.sqrt(pivot)
-        low_row = jnp.where(lane_row >= k, row, 0.0) / root
-        low_col = jnp.where(sub_col >= k, col, 0.0) / root
-        x_row = jnp.sum(jnp.where(sub == k, x, 0.0), axis=0, keepdims=True) / root
+        scale = 1.0 / jnp.sqrt(pivot)
+        low_row = jnp.where(lane_row >= k, row, 0.0) * scale
+        low_col = jnp.where(sub_col >= k, col, 0.0) * scale
+        x_row = jnp.sum(jnp.where(sub == k, x, 0.0), axis=0, keepdims=True) * scale
         a = a - low_col * low_row
         x = jnp.where(sub == k, x_row, x - jnp.where(sub_col > k, low_col, 0.0) * x_row)
         return a, x

time: 145 us -> 145 us (level)
  no operation moved by 1% of the time
where the time goes in v2:
time: 145 us; the launch traced here: 142 us
  Pallas kernels  61.6 us (42%)
  starting transfers between devices  25.2 us (17%)
  matrix products  23.1 us (16%)
  waiting for transfers between devices  18.3 us (13%)
  local copies, waits for them, and re-layouts  9.72 us (7%)
  other arithmetic  3.24 us (2%)
    pallas_call x2, Pallas kernels, lower_inverse_call(): pl.pallas_call(functools.partial(inverse_kernel, size=size), out_shape=ja...  37.3 us
    dot_general x10, matrix products, hdot(): return jnp.dot(a, b, precision=lax.Precision.HIGHEST)  23.1 us
    pallas_call x2, Pallas kernels, substep_call(): pl.pallas_call(functools.partial(substep_kernel, count=count, rows=rows,...  20 us
    ppermute x10, waiting for transfers between devices, exchange_sum(): array = array + lax.ppermute(array, axis, pairs)  16 us
    ppermute x8, starting transfers between devices, neighbour(): return lax.ppermute(array, axis, pairs)  14.4 us
    ppermute x10, starting transfers between devices, exchange_sum(): array = array + lax.ppermute(array, axis, pairs)  10.8 us
    unnamed x39, local copies, waits for them, and re-layouts  7.59 us
    pallas_call x1, Pallas kernels, edges_call(): pl.pallas_call(functools.partial(edges_kernel, count=count, rows=rows, co...  4.3 us
  transfers between devices with their start and end apart: 18, of which 6 were waited for; matrix products, arithmetic and copies ran while one was open for 16% of the time, Pallas kernels for 27%

profile of v2, /device:TPU:0, one launch (start us, length us, event | category | flops | bytes accessed | tf_op | source)
XLA Modules:
  0.0 142.5 jit_solution(14188175230297165408)
XLA Ops:
  0.6 0.0 copy-start
  0.6 4.3 %shard_map.69 = (f32[128,128]{1,0:T(8,128)}, f32[128,128]{1,0:T(8,128)}, f32[128,32]{1,0:T(8,128)}, f32[128,32]{1,0:T(8,128)}) custom-call(f32[4096,128]{1,0:T(8,128)} %bitcast.41), custom_call_target="tpu_custom_call" | custom-call | tf_op jit(solution)/shard_map/pallas_call | solution.py:73
  4.9 2.9 %collective-permute-start.5 = (f32[128,128]{1,0:T(8,128)}, f32[128,128]{1,0:T(8,128)S(1)}, u32[]{:S(2)}, u32[]{:S(2)}) collective-permute-start(f32[128,128]{1,0:T(8,128)} %get-tuple-element.12), channel_id=1, source_target_pairs={{0,8},{8,16},{16,24},{24,0},{1,9},{9,17},{17,25},{25,1},{2,10},{10... | collective-permute-start | bytes 196616 | tf_op jit(solution)/shard_map/ppermute | solution.py:13
  7.9 1.0 collective-permute-start.6
  8.8 4.0 %collective-permute-start.8 = (f32[128,32]{1,0:T(8,128)}, f32[128,32]{1,0:T(8,128)S(1)}, u32[]{:S(2)}, u32[]{:S(2)}) collective-permute-start(f32[128,32]{1,0:T(8,128)} %get-tuple-element.15), channel_id=1, source_target_pairs={{0,7},{1,0},{2,1},{3,2},{4,3},{5,4},{6,5},{7,6},{8,15},{9,8},{10,9... | collective-permute-start | bytes 49160 | tf_op jit(solution)/shard_map/ppermute | solution.py:13
  12.9 1.7 %copy.22 = f32[16,8,32,128]{3,1,2,0:T(8,128)S(1)} copy(f32[16,8,32,128]{3,2,1,0:T(8,128)S(1)} %bitcast.43) | data formatting | bytes 4194304
  14.6 1.6 %copy.23 = f32[16,8,32,128]{3,1,2,0:T(8,128)S(1)} copy(f32[16,8,32,128]{3,2,1,0:T(8,128)S(1)} %bitcast.45) | data formatting | bytes 4194304
  16.2 0.0 copy-start.15
  16.3 0.0 copy-start.16
  16.3 3.4 %fusion.10 = f32[128,256]{0,1:T(8,128)S(1)} fusion(f32[128,4096]{1,0:T(8,128)S(1)} %bitcast.48, f32[128,4096]{1,0:T(8,128)S(1)} %bitcast.46), kind=kOutput, calls=%fused_computation.14 | convolution fusion | flops 1611661312 | bytes 4325376 | tf_op jit(solution)/shard_map/dot_general | solution.py:113
  19.7 0.1 collective-permute-start
  19.8 0.1 copy.9
  19.9 0.1 copy.8
  20.0 0.7 pad_maximum_fusion.mix_ref
  20.7 0.0 collective-permute-done.5.above_ref
  20.7 0.6 copy-done.9
  21.3 0.0 copy-done.10
  21.3 0.0 copy-done.7
  21.4 0.0 copy-done.8
  21.4 10.1 %shard_map.70 = (f32[4096,128]{1,0:T(8,128)}, f32[128,128]{1,0:T(8,128)}, f32[128,128]{1,0:T(8,128)}, f32[128,32]{1,0:T(8,128)}, f32[128,32]{1,0:T(8,128)}) custom-call(f32[4096,128]{1,0:T(8,128)} %bitcast.42, f32[128,128]{1,0:T(8,128)} %copy-done.7, f32[128,128]{1,0:T(8,128)} %copy-done.8, f32[128,32]{1,0:T(8,128)} %copy-done.9, f32[128,32]{1,0:T(8,128)} %copy-done.10, ...), custom_call_target="tpu_custom_call" | custom-call | tf_op jit(solution)/shard_map/pallas_call | solution.py:83
  31.4 1.1 collective-permute-start.9
  32.5 1.9 %collective-permute-start.10 = (f32[128,128]{1,0:T(8,128)}, f32[128,128]{1,0:T(8,128)S(1)}, u32[]{:S(2)}, u32[]{:S(2)}) collective-permute-start(f32[128,128]{1,0:T(8,128)} %get-tuple-element.18), channel_id=1, source_target_pairs={{0,24},{8,0},{16,8},{24,16},{1,25},{9,1},{17,9},{25,17},{2,26},{10... | collective-permute-start | bytes 196616 | tf_op jit(solution)/shard_map/ppermute | solution.py:13
  34.4 0.0 collective-permute-start.11
  34.4 3.5 %collective-permute-start.12 = (f32[128,32]{1,0:T(8,128)}, f32[128,32]{1,0:T(8,128)S(1)}, u32[]{:S(2)}, u32[]{:S(2)}) collective-permute-start(f32[128,32]{1,0:T(8,128)} %get-tuple-element.20), channel_id=1, source_target_pairs={{0,7},{1,0},{2,1},{3,2},{4,3},{5,4},{6,5},{7,6},{8,15},{9,8},{10,9... | collective-permute-start | bytes 49160 | tf_op jit(solution)/shard_map/ppermute | solution.py:13
  37.9 2.3 %collective-permute-done.11.left_ref = f32[128,32]{1,0:T(8,128)S(1)} collective-permute-done((f32[128,32]{1,0:T(8,128)}, f32[128,32]{1,0:T(8,128)S(1)}, u32[]{:S(2)}, u32[]{:S(2)}) %collective-permute-start.11) | collective-permute-done | bytes 16416 | tf_op jit(solution)/shard_map/ppermute | solution.py:13
  40.2 0.0 collective-permute-done.9.above_ref
  40.2 0.6 copy-done.13
  40.8 0.0 copy-done.14
  40.8 0.0 copy-done.11
  40.9 10.0 %shard_map.71 = (f32[4096,128]{1,0:T(8,128)}, f32[128,128]{1,0:T(8,128)}, f32[128,128]{1,0:T(8,128)}, f32[128,32]{1,0:T(8,128)}, f32[128,32]{1,0:T(8,128)}) custom-call(f32[4096,128]{1,0:T(8,128)} %get-tuple-element.16.f_ref, f32[128,128]{1,0:T(8,128)} %copy-done.11, f32[128,128]{1,0:T(8,128)} %copy-done.12, f32[128,32]{1,0:T(8,128)} %copy-done.13, ...), custom_call_target="tpu_custom_call" | custom-call | tf_op jit(solution)/shard_map/pallas_call | solution.py:83
  50.8 1.9 %reshape.26 = f32[128,4096]{1,0:T(8,128)S(1)} reshape(f32[4096,128]{1,0:T(8,128)} %get-tuple-element.21) | data formatting | bytes 4194304 | tf_op jit(solution)/shard_map/reshape | solution.py:171
  52.8 0.0 copy-start.1
  52.8 0.1 collective-permute-start.1
  52.9 8.3 %fusion = f32[128,384]{0,1:T(8,128)S(1)} fusion(f32[128,4096]{1,0:T(8,128)S(1)} %reshape.26, f32[128,4096]{1,0:T(8,128)} %bitcast.47, f32[128,4096]{1,0:T(8,128)} %bitcast.49), kind=kOutput, calls=%fused_computation | convolution fusion | flops 2419064832 | bytes 6488064 | tf_op jit(solution)/shard_map/dot_general | solution.py:113
  61.2 0.1 collective-permute-start.13
  61.3 3.5 %collective-permute-start.2 = (f32[128,256]{0,1:T(8,128)S(1)}, f32[128,256]{0,1:T(8,128)S(1)}, u32[]{:S(2)}, u32[]{:S(2)}) collective-permute-start(f32[128,256]{0,1:T(8,128)S(1)} %add.37), channel_id=1, source_target_pairs={{0,4},{1,5},{2,6},{3,7},{4,0},{5,1},{6,2},{7,3},{8,12},{9,13},{10,... | collective-permute-start | bytes 393224 | tf_op jit(solution)/shard_map/ppermute | solution.py:107
  64.8 6.5 %collective-permute-done.2 = f32[128,256]{0,1:T(8,128)S(1)} collective-permute-done((f32[128,256]{0,1:T(8,128)S(1)}, f32[128,256]{0,1:T(8,128)S(1)}, u32[]{:S(2)}, u32[]{:S(2)}) %collective-permute-start.2) | collective-permute-done | bytes 131104 | tf_op jit(solution)/shard_map/ppermute | solution.py:107
  71.3 0.6 collective-permute-start.3
  71.9 0.3 collective-permute-start.14
  72.2 4.1 %collective-permute-done.3 = f32[128,256]{0,1:T(8,128)S(1)} collective-permute-done((f32[128,256]{0,1:T(8,128)S(1)}, f32[128,256]{0,1:T(8,128)S(1)}, u32[]{:S(2)}, u32[]{:S(2)}) %collective-permute-start.3) | collective-permute-done | bytes 131104 | tf_op jit(solution)/shard_map/ppermute | solution.py:107
  76.3 2.1 %collective-permute-start.4 = (f32[128,256]{0,1:T(8,128)S(1)}, f32[128,256]{0,1:T(8,128)S(1)}, u32[]{:S(2)}, u32[]{:S(2)}) collective-permute-start(f32[128,256]{0,1:T(8,128)S(1)} %add.39), channel_id=1, source_target_pairs={{0,16},{8,24},{16,0},{24,8},{1,17},{9,25},{17,1},{25,9},{2,18},{10... | collective-permute-start | bytes 393224 | tf_op jit(solution)/shard_map/ppermute | solution.py:107
  78.4 1.5 %collective-permute-start.15 = (f32[128,384]{0,1:T(8,128)S(1)}, f32[128,384]{0,1:T(8,128)S(1)}, u32[]{:S(2)}, u32[]{:S(2)}) collective-permute-start(f32[128,384]{0,1:T(8,128)S(1)} %add.43), channel_id=1, source_target_pairs={{0,4},{1,5},{2,6},{3,7},{4,0},{5,1},{6,2},{7,3},{8,12},{9,13},{10,... | collective-permute-start | bytes 589832 | tf_op jit(solution)/shard_map/ppermute | solution.py:107
  79.9 1.4 %collective-permute-done.4 = f32[128,256]{0,1:T(8,128)S(1)} collective-permute-done((f32[128,256]{0,1:T(8,128)S(1)}, f32[128,256]{0,1:T(8,128)S(1)}, u32[]{:S(2)}, u32[]{:S(2)}) %collective-permute-start.4) | collective-permute-done | bytes 131104 | tf_op jit(solution)/shard_map/ppermute | solution.py:107
  81.4 0.1 copy.7
  81.5 0.6 fusion.19.a_ref
  82.2 18.6 %shard_map.68 = f32[128,128]{1,0:T(8,128)} custom-call(f32[128,128]{1,0:T(8,128)} %fusion.19.a_ref), custom_call_target="tpu_custom_call" | custom-call | tf_op jit(solution)/shard_map/pallas_call | solution.py:143
  100.8 0.6 collective-permute-start.16
  101.4 4.6 %fusion.22 = f32[128,4096]{1,0:T(8,128)S(1)} fusion(f32[128,128]{1,0:T(8,128)} %shard_map.68, f32[16,8,32,128]{3,2,1,0:T(8,128)} %bitcast.44), kind=kOutput, calls=%fused_computation.33 | convolution fusion | flops 805306368 | bytes 4259840 | tf_op jit(solution)/shard_map/dot_general | solution.py:113
  106.0 0.5 collective-permute-done.16
  106.6 2.1 %collective-permute-start.17 = (f32[128,384]{0,1:T(8,128)S(1)}, f32[128,384]{0,1:T(8,128)S(1)}, u32[]{:S(2)}, u32[]{:S(2)}) collective-permute-start(f32[128,384]{0,1:T(8,128)S(1)} %add.45), channel_id=1, source_target_pairs={{0,16},{8,24},{16,0},{24,8},{1,17},{9,25},{17,1},{25,9},{2,18},{10... | collective-permute-start | bytes 589832 | tf_op jit(solution)/shard_map/ppermute | solution.py:107
  108.7 0.3 fusion.14
  108.9 3.4 %collective-permute-done.17 = f32[128,384]{0,1:T(8,128)S(1)} collective-permute-done((f32[128,384]{0,1:T(8,128)S(1)}, f32[128,384]{0,1:T(8,128)S(1)}, u32[]{:S(2)}, u32[]{:S(2)}) %collective-permute-start.17) | collective-permute-done | bytes 196640 | tf_op jit(solution)/shard_map/ppermute | solution.py:107
  112.4 0.3 fusion.16
  112.7 0.3 slice_subtract_fusion.2
  112.9 0.1 copy.13
  113.0 0.6 fusion.18.a_ref
  113.7 18.6 %shard_map.72 = f32[128,128]{1,0:T(8,128)} custom-call(f32[128,128]{1,0:T(8,128)} %fusion.18.a_ref), custom_call_target="tpu_custom_call" | custom-call | tf_op jit(solution)/shard_map/pallas_call | solution.py:143
  132.3 3.6 %convolution_subtract_fusion = f32[128,4096]{1,0:T(8,128)S(1)} fusion(f32[128,4096]{1,0:T(8,128)} %copy-done.1, f32[128,128]{1,0:T(8,128)S(1)} %fusion.16, f32[128,4096]{1,0:T(8,128)S(1)} %fusion.22), kind=kOutput, calls=%fused_computation.6 | convolution fusion | flops 805830656 | bytes 6356992 | tf_op jit(solution)/shard_map/dot_general | solution.py:113
  135.9 1.9 %fusion.23 = f32[128,4096]{1,0:T(8,128)S(1)} fusion(f32[128,128]{1,0:T(8,128)S(1)} %copy-done.6, f32[128,4096]{1,0:T(8,128)S(1)} %convolution_subtract_fusion), kind=kOutput, calls=%fused_computation.34 | convolution fusion | flops 805306368 | bytes 4259840 | tf_op jit(solution)/shard_map/dot_general | solution.py:113
  137.8 0.4 maximum_bitcast_fusion
  138.2 2.8 %copy.18 = f32[32,8,32,128]{3,2,1,0:T(8,128)} copy(f32[32,8,32,128]{3,1,2,0:T(8,128)S(1)} %maximum_bitcast_fusion) | data formatting | bytes 8388608
  141.0 0.3 fusion.24
  141.3 0.3 fusion.13
  141.5 0.7 pad_maximum_fusion.1
  (46 shorter events, 0.3 us)
Async XLA Ops:
  0.6 12.3 %copy-start = (f32[128,32,128]{2,1,0:T(8,128)S(1)}, f32[128,32,128]{2,1,0:T(8,128)}, u32[]{:S(2)}) copy-start(f32[128,32,128]{2,1,0:T(8,128)} %param.6) | copy-start | bytes 6291460
  4.9 15.7 %collective-permute-start.5 = (f32[128,128]{1,0:T(8,128)}, f32[128,128]{1,0:T(8,128)S(1)}, u32[]{:S(2)}, u32[]{:S(2)}) collective-permute-start(f32[128,128]{1,0:T(8,128)} %get-tuple-element.12), channel_id=1, source_target_pairs={{0,8},{8,16},{16,24},{24,0},{1,9},{9,17},{17,25},{25,1},{2,10},{10... | collective-permute-start | bytes 196616 | tf_op jit(solution)/shard_map/ppermute | solution.py:13
  7.9 12.8 %collective-permute-start.6 = (f32[128,128]{1,0:T(8,128)}, f32[128,128]{1,0:T(8,128)S(1)}, u32[]{:S(2)}, u32[]{:S(2)}) collective-permute-start(f32[128,128]{1,0:T(8,128)} %get-tuple-element.13), channel_id=1, source_target_pairs={{0,24},{8,0},{16,8},{24,16},{1,25},{9,1},{17,9},{25,17},{2,26},{10... | collective-permute-start | bytes 196616 | tf_op jit(solution)/shard_map/ppermute | solution.py:13
  8.8 11.8 %collective-permute-start.7 = (f32[128,32]{1,0:T(8,128)}, f32[128,32]{1,0:T(8,128)S(1)}, u32[]{:S(2)}, u32[]{:S(2)}) collective-permute-start(f32[128,32]{1,0:T(8,128)} %get-tuple-element.14), channel_id=1, source_target_pairs={{0,1},{1,2},{2,3},{3,4},{4,5},{5,6},{6,7},{7,0},{8,9},{9,10},{10,1... | collective-permute-start | bytes 49160 | tf_op jit(solution)/shard_map/ppermute | solution.py:13
  8.8 11.8 %collective-permute-start.8 = (f32[128,32]{1,0:T(8,128)}, f32[128,32]{1,0:T(8,128)S(1)}, u32[]{:S(2)}, u32[]{:S(2)}) collective-permute-start(f32[128,32]{1,0:T(8,128)} %get-tuple-element.15), channel_id=1, source_target_pairs={{0,7},{1,0},{2,1},{3,2},{4,3},{5,4},{6,5},{7,6},{8,15},{9,8},{10,9... | collective-permute-start | bytes 49160 | tf_op jit(solution)/shard_map/ppermute | solution.py:13
  12.9 1.7 %copy-start.2 = (f32[128,32,128]{2,1,0:T(8,128)S(1)}, f32[128,32,128]{2,1,0:T(8,128)}, u32[]{:S(2)}) copy-start(f32[128,32,128]{2,1,0:T(8,128)} %param.5) | copy-start | bytes 6291460
  14.6 1.7 %copy-start.3 = (f32[16,8,32,128]{3,1,2,0:T(8,128)}, f32[16,8,32,128]{3,1,2,0:T(8,128)S(1)}, u32[]{:S(2)}) copy-start(f32[16,8,32,128]{3,1,2,0:T(8,128)S(1)} %copy.22) | copy-start | bytes 6291460
  16.2 3.5 %copy-start.4 = (f32[16,8,32,128]{3,1,2,0:T(8,128)}, f32[16,8,32,128]{3,1,2,0:T(8,128)S(1)}, u32[]{:S(2)}) copy-start(f32[16,8,32,128]{3,1,2,0:T(8,128)S(1)} %copy.23) | copy-start | bytes 6291460
  16.2 3.5 %copy-start.15 = (f32[128,128]{1,0:T(8,128)S(1)}, f32[128,128]{1,0:T(8,128)}, u32[]{:S(2)}) copy-start(f32[128,128]{1,0:T(8,128)} %param.9) | copy-start | bytes 196612
  16.3 3.6 %copy-start.16 = (f32[128,128]{1,0:T(8,128)S(1)}, f32[128,128]{1,0:T(8,128)}, u32[]{:S(2)}) copy-start(f32[128,128]{1,0:T(8,128)} %param.8) | copy-start | bytes 196612
  19.7 33.1 %collective-permute-start = (f32[128,256]{0,1:T(8,128)S(1)}, f32[128,256]{0,1:T(8,128)S(1)}, u32[]{:S(2)}, u32[]{:S(2)}) collective-permute-start(f32[128,256]{0,1:T(8,128)S(1)} %fusion.10), channel_id=1, source_target_pairs={{0,1},{1,0},{2,3},{3,2},{4,5},{5,4},{6,7},{7,6},{8,9},{9,8},{10,11... | collective-permute-start | bytes 393224 | tf_op jit(solution)/shard_map/ppermute | solution.py:107
  20.7 0.6 copy-start.9
  20.7 0.6 copy-start.10
  20.7 0.7 copy-start.7
  20.7 0.7 copy-start.8
  31.4 8.7 %collective-permute-start.9 = (f32[128,128]{1,0:T(8,128)}, f32[128,128]{1,0:T(8,128)S(1)}, u32[]{:S(2)}, u32[]{:S(2)}) collective-permute-start(f32[128,128]{1,0:T(8,128)} %get-tuple-element.17), channel_id=1, source_target_pairs={{0,8},{8,16},{16,24},{24,0},{1,9},{9,17},{17,25},{25,1},{2,10},{10... | collective-permute-start | bytes 196616 | tf_op jit(solution)/shard_map/ppermute | solution.py:13
  32.5 7.7 %collective-permute-start.10 = (f32[128,128]{1,0:T(8,128)}, f32[128,128]{1,0:T(8,128)S(1)}, u32[]{:S(2)}, u32[]{:S(2)}) collective-permute-start(f32[128,128]{1,0:T(8,128)} %get-tuple-element.18), channel_id=1, source_target_pairs={{0,24},{8,0},{16,8},{24,16},{1,25},{9,1},{17,9},{25,17},{2,26},{10... | collective-permute-start | bytes 196616 | tf_op jit(solution)/shard_map/ppermute | solution.py:13
  34.4 5.8 %collective-permute-start.11 = (f32[128,32]{1,0:T(8,128)}, f32[128,32]{1,0:T(8,128)S(1)}, u32[]{:S(2)}, u32[]{:S(2)}) collective-permute-start(f32[128,32]{1,0:T(8,128)} %get-tuple-element.19), channel_id=1, source_target_pairs={{0,1},{1,2},{2,3},{3,4},{4,5},{5,6},{6,7},{7,0},{8,9},{9,10},{10,1... | collective-permute-start | bytes 49160 | tf_op jit(solution)/shard_map/ppermute | solution.py:13
  34.4 5.8 %collective-permute-start.12 = (f32[128,32]{1,0:T(8,128)}, f32[128,32]{1,0:T(8,128)S(1)}, u32[]{:S(2)}, u32[]{:S(2)}) collective-permute-start(f32[128,32]{1,0:T(8,128)} %get-tuple-element.20), channel_id=1, source_target_pairs={{0,7},{1,0},{2,1},{3,2},{4,3},{5,4},{6,5},{7,6},{8,15},{9,8},{10,9... | collective-permute-start | bytes 49160 | tf_op jit(solution)/shard_map/ppermute | solution.py:13
  40.2 0.6 copy-start.13
  40.2 0.7 copy-start.14
  40.2 0.7 copy-start.11
  40.2 0.7 copy-start.12
  52.8 8.4 %copy-start.1 = (f32[128,4096]{1,0:T(8,128)}, f32[128,4096]{1,0:T(8,128)S(1)}, u32[]{:S(2)}) copy-start(f32[128,4096]{1,0:T(8,128)S(1)} %reshape.26) | copy-start | bytes 6291460
  52.8 8.4 %collective-permute-start.1 = (f32[128,256]{0,1:T(8,128)S(1)}, f32[128,256]{0,1:T(8,128)S(1)}, u32[]{:S(2)}, u32[]{:S(2)}) collective-permute-start(f32[128,256]{0,1:T(8,128)S(1)} %add.36), channel_id=1, source_target_pairs={{0,2},{1,3},{2,0},{3,1},{4,6},{5,7},{6,4},{7,5},{8,10},{9,11},{10,... | collective-permute-start | bytes 393224 | tf_op jit(solution)/shard_map/ppermute | solution.py:107
  61.2 10.7 %collective-permute-start.13 = (f32[128,384]{0,1:T(8,128)S(1)}, f32[128,384]{0,1:T(8,128)S(1)}, u32[]{:S(2)}, u32[]{:S(2)}) collective-permute-start(f32[128,384]{0,1:T(8,128)S(1)} %fusion), channel_id=1, source_target_pairs={{0,1},{1,0},{2,3},{3,2},{4,5},{5,4},{6,7},{7,6},{8,9},{9,8},{10,11... | collective-permute-start | bytes 589832 | tf_op jit(solution)/shard_map/ppermute | solution.py:107
  61.3 10.0 %collective-permute-start.2 = (f32[128,256]{0,1:T(8,128)S(1)}, f32[128,256]{0,1:T(8,128)S(1)}, u32[]{:S(2)}, u32[]{:S(2)}) collective-permute-start(f32[128,256]{0,1:T(8,128)S(1)} %add.37), channel_id=1, source_target_pairs={{0,4},{1,5},{2,6},{3,7},{4,0},{5,1},{6,2},{7,3},{8,12},{9,13},{10,... | collective-permute-start | bytes 393224 | tf_op jit(solution)/shard_map/ppermute | solution.py:107
  71.3 5.0 %collective-permute-start.3 = (f32[128,256]{0,1:T(8,128)S(1)}, f32[128,256]{0,1:T(8,128)S(1)}, u32[]{:S(2)}, u32[]{:S(2)}) collective-permute-start(f32[128,256]{0,1:T(8,128)S(1)} %add.38), channel_id=1, source_target_pairs={{0,8},{8,0},{16,24},{24,16},{1,9},{9,1},{17,25},{25,17},{2,10},{10... | collective-permute-start | bytes 393224 | tf_op jit(solution)/shard_map/ppermute | solution.py:107
  71.9 6.5 %collective-permute-start.14 = (f32[128,384]{0,1:T(8,128)S(1)}, f32[128,384]{0,1:T(8,128)S(1)}, u32[]{:S(2)}, u32[]{:S(2)}) collective-permute-start(f32[128,384]{0,1:T(8,128)S(1)} %add.42), channel_id=1, source_target_pairs={{0,2},{1,3},{2,0},{3,1},{4,6},{5,7},{6,4},{7,5},{8,10},{9,11},{10,... | collective-permute-start | bytes 589832 | tf_op jit(solution)/shard_map/ppermute | solution.py:107
  76.3 5.0 %collective-permute-start.4 = (f32[128,256]{0,1:T(8,128)S(1)}, f32[128,256]{0,1:T(8,128)S(1)}, u32[]{:S(2)}, u32[]{:S(2)}) collective-permute-start(f32[128,256]{0,1:T(8,128)S(1)} %add.39), channel_id=1, source_target_pairs={{0,16},{8,24},{16,0},{24,8},{1,17},{9,25},{17,1},{25,9},{2,18},{10... | collective-permute-start | bytes 393224 | tf_op jit(solution)/shard_map/ppermute | solution.py:107
  78.4 22.4 %collective-permute-start.15 = (f32[128,384]{0,1:T(8,128)S(1)}, f32[128,384]{0,1:T(8,128)S(1)}, u32[]{:S(2)}, u32[]{:S(2)}) collective-permute-start(f32[128,384]{0,1:T(8,128)S(1)} %add.43), channel_id=1, source_target_pairs={{0,4},{1,5},{2,6},{3,7},{4,0},{5,1},{6,2},{7,3},{8,12},{9,13},{10,... | collective-permute-start | bytes 589832 | tf_op jit(solution)/shard_map/ppermute | solution.py:107
  100.8 7.8 %copy-start.5 = (f32[128,128]{1,0:T(8,128)S(1)}, f32[128,128]{1,0:T(8,128)}, u32[]{:S(2)}) copy-start(f32[128,128]{1,0:T(8,128)} %shard_map.68) | copy-start | bytes 196612
  100.8 5.7 %collective-permute-start.16 = (f32[128,384]{0,1:T(8,128)S(1)}, f32[128,384]{0,1:T(8,128)S(1)}, u32[]{:S(2)}, u32[]{:S(2)}) collective-permute-start(f32[128,384]{0,1:T(8,128)S(1)} %add.44), channel_id=1, source_target_pairs={{0,8},{8,0},{16,24},{24,16},{1,9},{9,1},{17,25},{25,17},{2,10},{10... | collective-permute-start | bytes 589832 | tf_op jit(solution)/shard_map/ppermute | solution.py:107
  106.6 5.7 %collective-permute-start.17 = (f32[128,384]{0,1:T(8,128)S(1)}, f32[128,384]{0,1:T(8,128)S(1)}, u32[]{:S(2)}, u32[]{:S(2)}) collective-permute-start(f32[128,384]{0,1:T(8,128)S(1)} %add.45), channel_id=1, source_target_pairs={{0,16},{8,24},{16,0},{24,8},{1,17},{9,25},{17,1},{25,9},{2,18},{10... | collective-permute-start | bytes 589832 | tf_op jit(solution)/shard_map/ppermute | solution.py:107
  132.3 3.6 %copy-start.6 = (f32[128,128]{1,0:T(8,128)S(1)}, f32[128,128]{1,0:T(8,128)}, u32[]{:S(2)}) copy-start(f32[128,128]{1,0:T(8,128)} %shard_map.72) | copy-start | bytes 196612

commit v3 on v2

--- a/solution.py
+++ b/solution.py
@@ -119,21 +119,33 @@
     lane_row = lax.broadcasted_iota(jnp.int32, (1, size), 1)
     sub_col = lax.broadcasted_iota(jnp.int32, (size, 1), 0)
 
+    def row_at(m, k):
+        return jnp.sum(jnp.where(sub == k, m, 0.0), axis=0, keepdims=True)
+
+    def col_at(m, k):
+        return jnp.sum(jnp.where(lane == k, m, 0.0), axis=1, keepdims=True)
+
+    def lane_at(v, k):
+        return jnp.sum(jnp.where(lane_row == k, v, 0.0), axis=1, keepdims=True)
+
     def step(k, carry):
-        a, x = carry
-        row = jnp.sum(jnp.where(sub == k, a, 0.0), axis=0, keepdims=True)
-        col = jnp.sum(jnp.where(lane == k, a, 0.0), axis=1, keepdims=True)
-        pivot = jnp.sum(jnp.where(lane_row == k, row, 0.0), axis=1, keepdims=True)
-        scale = 1.0 / jnp.sqrt(pivot)
+        a, x, row, col, x_raw = carry
+        scale = 1.0 / jnp.sqrt(lane_at(row, k))
+        cross = lane_at(row, k + 1) * scale
         low_row = jnp.where(lane_row >= k, row, 0.0) * scale
         low_col = jnp.where(sub_col >= k, col, 0.0) * scale
-        x_row = jnp.sum(jnp.where(sub == k, x, 0.0), axis=0, keepdims=True) * scale
+        x_row = x_raw * scale
+        next_row = row_at(a, k + 1) - cross * low_row
+        next_col = col_at(a, k + 1) - cross * low_col
+        next_x = row_at(x, k + 1) - cross * x_row
         a = a - low_col * low_row
         x = jnp.where(sub == k, x_row, x - jnp.where(sub_col > k, low_col, 0.0) * x_row)
-        return a, x
-
+        return a, x, next_row, next_col, next_x
+
+    a0 = a_ref[...]
     eye = jnp.where(sub == lane, 1.0, 0.0).astype(jnp.float32)
-    _, x = lax.fori_loop(0, size, step, (a_ref[...], eye), unroll=4)
+    init = (a0, eye, row_at(a0, 0), col_at(a0, 0), row_at(eye, 0))
+    x = lax.fori_loop(0, size, step, init, unroll=4)[1]
     x_ref[...] = x
 
 

time: 145 us -> 139 us (0.959)
  Pallas kernels: 61.6 us -> 55 us
    pallas_call x2, Pallas kernels: 37.3 us -> 30.6 us  [lower_inverse_call(): pl.pallas_call(functools.partial(inverse_kernel, size=size), out_shape=ja...]
  transfers between devices with their start and end apart: 18 -> 18, of which waited for: 6 -> 6; matrix products, arithmetic and copies ran while one was open for 16% -> 17% of each run, Pallas kernels for 27% -> 26%
where the time goes in v3:
time: 139 us; the launch traced here: 136 us
  Pallas kernels  55 us (40%)
  starting transfers between devices  25.2 us (18%)
  matrix products  23.1 us (17%)
  waiting for transfers between devices  18.3 us (13%)
  local copies, waits for them, and re-layouts  9.72 us (7%)
  other arithmetic  3.24 us (2%)
    pallas_call x2, Pallas kernels, lower_inverse_call(): pl.pallas_call(functools.partial(inverse_kernel, size=size), out_shape=ja...  30.6 us
    dot_general x10, matrix products, hdot(): return jnp.dot(a, b, precision=lax.Precision.HIGHEST)  23.1 us
    pallas_call x2, Pallas kernels, substep_call(): pl.pallas_call(functools.partial(substep_kernel, count=count, rows=rows,...  20 us
    ppermute x10, waiting for transfers between devices, exchange_sum(): array = array + lax.ppermute(array, axis, pairs)  16 us
    ppermute x8, starting transfers between devices, neighbour(): return lax.ppermute(array, axis, pairs)  14.4 us
    ppermute x10, starting transfers between devices, exchange_sum(): array = array + lax.ppermute(array, axis, pairs)  10.8 us
    unnamed x39, local copies, waits for them, and re-layouts  7.59 us
    pallas_call x1, Pallas kernels, edges_call(): pl.pallas_call(functools.partial(edges_kernel, count=count, rows=rows, co...  4.3 us
  transfers between devices with their start and end apart: 18, of which 6 were waited for; matrix products, arithmetic and copies ran while one was open for 17% of the time, Pallas kernels for 26%

profile of v3, /device:TPU:0, one launch (start us, length us, event | category | flops | bytes accessed | tf_op | source)
XLA Modules:
  0.0 135.8 jit_solution(2924764352972458372)
XLA Ops:
  0.6 0.0 copy-start
  0.6 4.3 %shard_map.69 = (f32[128,128]{1,0:T(8,128)}, f32[128,128]{1,0:T(8,128)}, f32[128,32]{1,0:T(8,128)}, f32[128,32]{1,0:T(8,128)}) custom-call(f32[4096,128]{1,0:T(8,128)} %bitcast.41), custom_call_target="tpu_custom_call" | custom-call | tf_op jit(solution)/shard_map/pallas_call | solution.py:73
  4.9 2.9 %collective-permute-start.5 = (f32[128,128]{1,0:T(8,128)}, f32[128,128]{1,0:T(8,128)S(1)}, u32[]{:S(2)}, u32[]{:S(2)}) collective-permute-start(f32[128,128]{1,0:T(8,128)} %get-tuple-element.12), channel_id=1, source_target_pairs={{0,8},{8,16},{16,24},{24,0},{1,9},{9,17},{17,25},{25,1},{2,10},{10... | collective-permute-start | bytes 196616 | tf_op jit(solution)/shard_map/ppermute | solution.py:13
  7.9 1.0 collective-permute-start.6
  8.8 4.0 %collective-permute-start.8 = (f32[128,32]{1,0:T(8,128)}, f32[128,32]{1,0:T(8,128)S(1)}, u32[]{:S(2)}, u32[]{:S(2)}) collective-permute-start(f32[128,32]{1,0:T(8,128)} %get-tuple-element.15), channel_id=1, source_target_pairs={{0,7},{1,0},{2,1},{3,2},{4,3},{5,4},{6,5},{7,6},{8,15},{9,8},{10,9... | collective-permute-start | bytes 49160 | tf_op jit(solution)/shard_map/ppermute | solution.py:13
  12.9 1.7 %copy.22 = f32[16,8,32,128]{3,1,2,0:T(8,128)S(1)} copy(f32[16,8,32,128]{3,2,1,0:T(8,128)S(1)} %bitcast.43) | data formatting | bytes 4194304
  14.6 1.6 %copy.23 = f32[16,8,32,128]{3,1,2,0:T(8,128)S(1)} copy(f32[16,8,32,128]{3,2,1,0:T(8,128)S(1)} %bitcast.45) | data formatting | bytes 4194304
  16.2 0.0 copy-start.15
  16.3 0.0 copy-start.16
  16.3 3.4 %fusion.10 = f32[128,256]{0,1:T(8,128)S(1)} fusion(f32[128,4096]{1,0:T(8,128)S(1)} %bitcast.48, f32[128,4096]{1,0:T(8,128)S(1)} %bitcast.46), kind=kOutput, calls=%fused_computation.14 | convolution fusion | flops 1611661312 | bytes 4325376 | tf_op jit(solution)/shard_map/dot_general | solution.py:113
  19.7 0.1 collective-permute-start
  19.8 0.1 copy.9
  19.9 0.1 copy.8
  20.0 0.7 pad_maximum_fusion.mix_ref
  20.7 0.0 collective-permute-done.5.above_ref
  20.7 0.6 copy-done.9
  21.3 0.0 copy-done.10
  21.3 0.0 copy-done.7
  21.4 0.0 copy-done.8
  21.4 10.1 %shard_map.70 = (f32[4096,128]{1,0:T(8,128)}, f32[128,128]{1,0:T(8,128)}, f32[128,128]{1,0:T(8,128)}, f32[128,32]{1,0:T(8,128)}, f32[128,32]{1,0:T(8,128)}) custom-call(f32[4096,128]{1,0:T(8,128)} %bitcast.42, f32[128,128]{1,0:T(8,128)} %copy-done.7, f32[128,128]{1,0:T(8,128)} %copy-done.8, f32[128,32]{1,0:T(8,128)} %copy-done.9, f32[128,32]{1,0:T(8,128)} %copy-done.10, ...), custom_call_target="tpu_custom_call" | custom-call | tf_op jit(solution)/shard_map/pallas_call | solution.py:83
  31.4 1.1 collective-permute-start.9
  32.5 1.9 %collective-permute-start.10 = (f32[128,128]{1,0:T(8,128)}, f32[128,128]{1,0:T(8,128)S(1)}, u32[]{:S(2)}, u32[]{:S(2)}) collective-permute-start(f32[128,128]{1,0:T(8,128)} %get-tuple-element.18), channel_id=1, source_target_pairs={{0,24},{8,0},{16,8},{24,16},{1,25},{9,1},{17,9},{25,17},{2,26},{10... | collective-permute-start | bytes 196616 | tf_op jit(solution)/shard_map/ppermute | solution.py:13
  34.4 0.0 collective-permute-start.11
  34.4 3.5 %collective-permute-start.12 = (f32[128,32]{1,0:T(8,128)}, f32[128,32]{1,0:T(8,128)S(1)}, u32[]{:S(2)}, u32[]{:S(2)}) collective-permute-start(f32[128,32]{1,0:T(8,128)} %get-tuple-element.20), channel_id=1, source_target_pairs={{0,7},{1,0},{2,1},{3,2},{4,3},{5,4},{6,5},{7,6},{8,15},{9,8},{10,9... | collective-permute-start | bytes 49160 | tf_op jit(solution)/shard_map/ppermute | solution.py:13
  37.9 2.3 %collective-permute-done.11.left_ref = f32[128,32]{1,0:T(8,128)S(1)} collective-permute-done((f32[128,32]{1,0:T(8,128)}, f32[128,32]{1,0:T(8,128)S(1)}, u32[]{:S(2)}, u32[]{:S(2)}) %collective-permute-start.11) | collective-permute-done | bytes 16416 | tf_op jit(solution)/shard_map/ppermute | solution.py:13
  40.2 0.0 collective-permute-done.9.above_ref
  40.2 0.6 copy-done.13
  40.8 0.0 copy-done.14
  40.8 0.0 copy-done.11
  40.9 10.0 %shard_map.71 = (f32[4096,128]{1,0:T(8,128)}, f32[128,128]{1,0:T(8,128)}, f32[128,128]{1,0:T(8,128)}, f32[128,32]{1,0:T(8,128)}, f32[128,32]{1,0:T(8,128)}) custom-call(f32[4096,128]{1,0:T(8,128)} %get-tuple-element.16.f_ref, f32[128,128]{1,0:T(8,128)} %copy-done.11, f32[128,128]{1,0:T(8,128)} %copy-done.12, f32[128,32]{1,0:T(8,128)} %copy-done.13, ...), custom_call_target="tpu_custom_call" | custom-call | tf_op jit(solution)/shard_map/pallas_call | solution.py:83
  50.8 1.9 %reshape.26 = f32[128,4096]{1,0:T(8,128)S(1)} reshape(f32[4096,128]{1,0:T(8,128)} %get-tuple-element.21) | data formatting | bytes 4194304 | tf_op jit(solution)/shard_map/reshape | solution.py:183
  52.8 0.0 copy-start.1
  52.8 0.1 collective-permute-start.1
  52.9 8.3 %fusion = f32[128,384]{0,1:T(8,128)S(1)} fusion(f32[128,4096]{1,0:T(8,128)S(1)} %reshape.26, f32[128,4096]{1,0:T(8,128)} %bitcast.47, f32[128,4096]{1,0:T(8,128)} %bitcast.49), kind=kOutput, calls=%fused_computation | convolution fusion | flops 2419064832 | bytes 6488064 | tf_op jit(solution)/shard_map/dot_general | solution.py:113
  61.2 0.1 collective-permute-start.13
  61.3 3.5 %collective-permute-start.2 = (f32[128,256]{0,1:T(8,128)S(1)}, f32[128,256]{0,1:T(8,128)S(1)}, u32[]{:S(2)}, u32[]{:S(2)}) collective-permute-start(f32[128,256]{0,1:T(8,128)S(1)} %add.37), channel_id=1, source_target_pairs={{0,4},{1,5},{2,6},{3,7},{4,0},{5,1},{6,2},{7,3},{8,12},{9,13},{10,... | collective-permute-start | bytes 393224 | tf_op jit(solution)/shard_map/ppermute | solution.py:107
  64.8 6.5 %collective-permute-done.2 = f32[128,256]{0,1:T(8,128)S(1)} collective-permute-done((f32[128,256]{0,1:T(8,128)S(1)}, f32[128,256]{0,1:T(8,128)S(1)}, u32[]{:S(2)}, u32[]{:S(2)}) %collective-permute-start.2) | collective-permute-done | bytes 131104 | tf_op jit(solution)/shard_map/ppermute | solution.py:107
  71.3 0.6 collective-permute-start.3
  71.9 0.3 collective-permute-start.14
  72.2 4.1 %collective-permute-done.3 = f32[128,256]{0,1:T(8,128)S(1)} collective-permute-done((f32[128,256]{0,1:T(8,128)S(1)}, f32[128,256]{0,1:T(8,128)S(1)}, u32[]{:S(2)}, u32[]{:S(2)}) %collective-permute-start.3) | collective-permute-done | bytes 131104 | tf_op jit(solution)/shard_map/ppermute | solution.py:107
  76.3 2.1 %collective-permute-start.4 = (f32[128,256]{0,1:T(8,128)S(1)}, f32[128,256]{0,1:T(8,128)S(1)}, u32[]{:S(2)}, u32[]{:S(2)}) collective-permute-start(f32[128,256]{0,1:T(8,128)S(1)} %add.39), channel_id=1, source_target_pairs={{0,16},{8,24},{16,0},{24,8},{1,17},{9,25},{17,1},{25,9},{2,18},{10... | collective-permute-start | bytes 393224 | tf_op jit(solution)/shard_map/ppermute | solution.py:107
  78.4 1.5 %collective-permute-start.15 = (f32[128,384]{0,1:T(8,128)S(1)}, f32[128,384]{0,1:T(8,128)S(1)}, u32[]{:S(2)}, u32[]{:S(2)}) collective-permute-start(f32[128,384]{0,1:T(8,128)S(1)} %add.43), channel_id=1, source_target_pairs={{0,4},{1,5},{2,6},{3,7},{4,0},{5,1},{6,2},{7,3},{8,12},{9,13},{10,... | collective-permute-start | bytes 589832 | tf_op jit(solution)/shard_map/ppermute | solution.py:107
  79.9 1.4 %collective-permute-done.4 = f32[128,256]{0,1:T(8,128)S(1)} collective-permute-done((f32[128,256]{0,1:T(8,128)S(1)}, f32[128,256]{0,1:T(8,128)S(1)}, u32[]{:S(2)}, u32[]{:S(2)}) %collective-permute-start.4) | collective-permute-done | bytes 131104 | tf_op jit(solution)/shard_map/ppermute | solution.py:107
  81.4 0.1 copy.7
  81.5 0.6 fusion.19.a_ref
  82.2 15.2 %shard_map.68 = f32[128,128]{1,0:T(8,128)} custom-call(f32[128,128]{1,0:T(8,128)} %fusion.19.a_ref), custom_call_target="tpu_custom_call" | custom-call | tf_op jit(solution)/shard_map/pallas_call | solution.py:155
  97.4 0.6 collective-permute-start.16
  98.0 4.6 %fusion.22 = f32[128,4096]{1,0:T(8,128)S(1)} fusion(f32[128,128]{1,0:T(8,128)} %shard_map.68, f32[16,8,32,128]{3,2,1,0:T(8,128)} %bitcast.44), kind=kOutput, calls=%fused_computation.33 | convolution fusion | flops 805306368 | bytes 4259840 | tf_op jit(solution)/shard_map/dot_general | solution.py:113
  102.6 0.5 collective-permute-done.16
  103.2 2.1 %collective-permute-start.17 = (f32[128,384]{0,1:T(8,128)S(1)}, f32[128,384]{0,1:T(8,128)S(1)}, u32[]{:S(2)}, u32[]{:S(2)}) collective-permute-start(f32[128,384]{0,1:T(8,128)S(1)} %add.45), channel_id=1, source_target_pairs={{0,16},{8,24},{16,0},{24,8},{1,17},{9,25},{17,1},{25,9},{2,18},{10... | collective-permute-start | bytes 589832 | tf_op jit(solution)/shard_map/ppermute | solution.py:107
  105.2 0.3 fusion.14
  105.5 3.4 %collective-permute-done.17 = f32[128,384]{0,1:T(8,128)S(1)} collective-permute-done((f32[128,384]{0,1:T(8,128)S(1)}, f32[128,384]{0,1:T(8,128)S(1)}, u32[]{:S(2)}, u32[]{:S(2)}) %collective-permute-start.17) | collective-permute-done | bytes 196640 | tf_op jit(solution)/shard_map/ppermute | solution.py:107
  108.9 0.3 fusion.16
  109.2 0.3 slice_subtract_fusion.2
  109.5 0.1 copy.13
  109.6 0.6 fusion.18.a_ref
  110.2 15.4 %shard_map.72 = f32[128,128]{1,0:T(8,128)} custom-call(f32[128,128]{1,0:T(8,128)} %fusion.18.a_ref), custom_call_target="tpu_custom_call" | custom-call | tf_op jit(solution)/shard_map/pallas_call | solution.py:155
  125.7 3.6 %convolution_subtract_fusion = f32[128,4096]{1,0:T(8,128)S(1)} fusion(f32[128,4096]{1,0:T(8,128)} %copy-done.1, f32[128,128]{1,0:T(8,128)S(1)} %fusion.16, f32[128,4096]{1,0:T(8,128)S(1)} %fusion.22), kind=kOutput, calls=%fused_computation.6 | convolution fusion | flops 805830656 | bytes 6356992 | tf_op jit(solution)/shard_map/dot_general | solution.py:113
  129.2 1.9 %fusion.23 = f32[128,4096]{1,0:T(8,128)S(1)} fusion(f32[128,128]{1,0:T(8,128)S(1)} %copy-done.6, f32[128,4096]{1,0:T(8,128)S(1)} %convolution_subtract_fusion), kind=kOutput, calls=%fused_computation.34 | convolution fusion | flops 805306368 | bytes 4259840 | tf_op jit(solution)/shard_map/dot_general | solution.py:113
  131.2 0.4 maximum_bitcast_fusion
  131.6 2.8 %copy.18 = f32[32,8,32,128]{3,2,1,0:T(8,128)} copy(f32[32,8,32,128]{3,1,2,0:T(8,128)S(1)} %maximum_bitcast_fusion) | data formatting | bytes 8388608
  134.3 0.3 fusion.24
  134.6 0.3 fusion.13
  134.9 0.7 pad_maximum_fusion.1
  (46 shorter events, 0.3 us)
Async XLA Ops:
  0.6 12.3 %copy-start = (f32[128,32,128]{2,1,0:T(8,128)S(1)}, f32[128,32,128]{2,1,0:T(8,128)}, u32[]{:S(2)}) copy-start(f32[128,32,128]{2,1,0:T(8,128)} %param.6) | copy-start | bytes 6291460
  4.9 15.7 %collective-permute-start.5 = (f32[128,128]{1,0:T(8,128)}, f32[128,128]{1,0:T(8,128)S(1)}, u32[]{:S(2)}, u32[]{:S(2)}) collective-permute-start(f32[128,128]{1,0:T(8,128)} %get-tuple-element.12), channel_id=1, source_target_pairs={{0,8},{8,16},{16,24},{24,0},{1,9},{9,17},{17,25},{25,1},{2,10},{10... | collective-permute-start | bytes 196616 | tf_op jit(solution)/shard_map/ppermute | solution.py:13
  7.9 12.8 %collective-permute-start.6 = (f32[128,128]{1,0:T(8,128)}, f32[128,128]{1,0:T(8,128)S(1)}, u32[]{:S(2)}, u32[]{:S(2)}) collective-permute-start(f32[128,128]{1,0:T(8,128)} %get-tuple-element.13), channel_id=1, source_target_pairs={{0,24},{8,0},{16,8},{24,16},{1,25},{9,1},{17,9},{25,17},{2,26},{10... | collective-permute-start | bytes 196616 | tf_op jit(solution)/shard_map/ppermute | solution.py:13
  8.8 11.8 %collective-permute-start.7 = (f32[128,32]{1,0:T(8,128)}, f32[128,32]{1,0:T(8,128)S(1)}, u32[]{:S(2)}, u32[]{:S(2)}) collective-permute-start(f32[128,32]{1,0:T(8,128)} %get-tuple-element.14), channel_id=1, source_target_pairs={{0,1},{1,2},{2,3},{3,4},{4,5},{5,6},{6,7},{7,0},{8,9},{9,10},{10,1... | collective-permute-start | bytes 49160 | tf_op jit(solution)/shard_map/ppermute | solution.py:13
  8.8 11.8 %collective-permute-start.8 = (f32[128,32]{1,0:T(8,128)}, f32[128,32]{1,0:T(8,128)S(1)}, u32[]{:S(2)}, u32[]{:S(2)}) collective-permute-start(f32[128,32]{1,0:T(8,128)} %get-tuple-element.15), channel_id=1, source_target_pairs={{0,7},{1,0},{2,1},{3,2},{4,3},{5,4},{6,5},{7,6},{8,15},{9,8},{10,9... | collective-permute-start | bytes 49160 | tf_op jit(solution)/shard_map/ppermute | solution.py:13
  12.9 1.7 %copy-start.2 = (f32[128,32,128]{2,1,0:T(8,128)S(1)}, f32[128,32,128]{2,1,0:T(8,128)}, u32[]{:S(2)}) copy-start(f32[128,32,128]{2,1,0:T(8,128)} %param.5) | copy-start | bytes 6291460
  14.6 1.7 %copy-start.3 = (f32[16,8,32,128]{3,1,2,0:T(8,128)}, f32[16,8,32,128]{3,1,2,0:T(8,128)S(1)}, u32[]{:S(2)}) copy-start(f32[16,8,32,128]{3,1,2,0:T(8,128)S(1)} %copy.22) | copy-start | bytes 6291460
  16.2 3.5 %copy-start.4 = (f32[16,8,32,128]{3,1,2,0:T(8,128)}, f32[16,8,32,128]{3,1,2,0:T(8,128)S(1)}, u32[]{:S(2)}) copy-start(f32[16,8,32,128]{3,1,2,0:T(8,128)S(1)} %copy.23) | copy-start | bytes 6291460
  16.2 3.5 %copy-start.15 = (f32[128,128]{1,0:T(8,128)S(1)}, f32[128,128]{1,0:T(8,128)}, u32[]{:S(2)}) copy-start(f32[128,128]{1,0:T(8,128)} %param.9) | copy-start | bytes 196612
  16.3 3.6 %copy-start.16 = (f32[128,128]{1,0:T(8,128)S(1)}, f32[128,128]{1,0:T(8,128)}, u32[]{:S(2)}) copy-start(f32[128,128]{1,0:T(8,128)} %param.8) | copy-start | bytes 196612
  19.7 33.1 %collective-permute-start = (f32[128,256]{0,1:T(8,128)S(1)}, f32[128,256]{0,1:T(8,128)S(1)}, u32[]{:S(2)}, u32[]{:S(2)}) collective-permute-start(f32[128,256]{0,1:T(8,128)S(1)} %fusion.10), channel_id=1, source_target_pairs={{0,1},{1,0},{2,3},{3,2},{4,5},{5,4},{6,7},{7,6},{8,9},{9,8},{10,11... | collective-permute-start | bytes 393224 | tf_op jit(solution)/shard_map/ppermute | solution.py:107
  20.7 0.6 copy-start.9
  20.7 0.6 copy-start.10
  20.7 0.7 copy-start.7
  20.7 0.7 copy-start.8
  31.4 8.7 %collective-permute-start.9 = (f32[128,128]{1,0:T(8,128)}, f32[128,128]{1,0:T(8,128)S(1)}, u32[]{:S(2)}, u32[]{:S(2)}) collective-permute-start(f32[128,128]{1,0:T(8,128)} %get-tuple-element.17), channel_id=1, source_target_pairs={{0,8},{8,16},{16,24},{24,0},{1,9},{9,17},{17,25},{25,1},{2,10},{10... | collective-permute-start | bytes 196616 | tf_op jit(solution)/shard_map/ppermute | solution.py:13
  32.5 7.7 %collective-permute-start.10 = (f32[128,128]{1,0:T(8,128)}, f32[128,128]{1,0:T(8,128)S(1)}, u32[]{:S(2)}, u32[]{:S(2)}) collective-permute-start(f32[128,128]{1,0:T(8,128)} %get-tuple-element.18), channel_id=1, source_target_pairs={{0,24},{8,0},{16,8},{24,16},{1,25},{9,1},{17,9},{25,17},{2,26},{10... | collective-permute-start | bytes 196616 | tf_op jit(solution)/shard_map/ppermute | solution.py:13
  34.4 5.8 %collective-permute-start.11 = (f32[128,32]{1,0:T(8,128)}, f32[128,32]{1,0:T(8,128)S(1)}, u32[]{:S(2)}, u32[]{:S(2)}) collective-permute-start(f32[128,32]{1,0:T(8,128)} %get-tuple-element.19), channel_id=1, source_target_pairs={{0,1},{1,2},{2,3},{3,4},{4,5},{5,6},{6,7},{7,0},{8,9},{9,10},{10,1... | collective-permute-start | bytes 49160 | tf_op jit(solution)/shard_map/ppermute | solution.py:13
  34.4 5.8 %collective-permute-start.12 = (f32[128,32]{1,0:T(8,128)}, f32[128,32]{1,0:T(8,128)S(1)}, u32[]{:S(2)}, u32[]{:S(2)}) collective-permute-start(f32[128,32]{1,0:T(8,128)} %get-tuple-element.20), channel_id=1, source_target_pairs={{0,7},{1,0},{2,1},{3,2},{4,3},{5,4},{6,5},{7,6},{8,15},{9,8},{10,9... | collective-permute-start | bytes 49160 | tf_op jit(solution)/shard_map/ppermute | solution.py:13
  40.2 0.6 copy-start.13
  40.2 0.7 copy-start.14
  40.2 0.7 copy-start.11
  40.2 0.7 copy-start.12
  52.8 8.4 %copy-start.1 = (f32[128,4096]{1,0:T(8,128)}, f32[128,4096]{1,0:T(8,128)S(1)}, u32[]{:S(2)}) copy-start(f32[128,4096]{1,0:T(8,128)S(1)} %reshape.26) | copy-start | bytes 6291460
  52.8 8.4 %collective-permute-start.1 = (f32[128,256]{0,1:T(8,128)S(1)}, f32[128,256]{0,1:T(8,128)S(1)}, u32[]{:S(2)}, u32[]{:S(2)}) collective-permute-start(f32[128,256]{0,1:T(8,128)S(1)} %add.36), channel_id=1, source_target_pairs={{0,2},{1,3},{2,0},{3,1},{4,6},{5,7},{6,4},{7,5},{8,10},{9,11},{10,... | collective-permute-start | bytes 393224 | tf_op jit(solution)/shard_map/ppermute | solution.py:107
  61.2 10.7 %collective-permute-start.13 = (f32[128,384]{0,1:T(8,128)S(1)}, f32[128,384]{0,1:T(8,128)S(1)}, u32[]{:S(2)}, u32[]{:S(2)}) collective-permute-start(f32[128,384]{0,1:T(8,128)S(1)} %fusion), channel_id=1, source_target_pairs={{0,1},{1,0},{2,3},{3,2},{4,5},{5,4},{6,7},{7,6},{8,9},{9,8},{10,11... | collective-permute-start | bytes 589832 | tf_op jit(solution)/shard_map/ppermute | solution.py:107
  61.3 10.0 %collective-permute-start.2 = (f32[128,256]{0,1:T(8,128)S(1)}, f32[128,256]{0,1:T(8,128)S(1)}, u32[]{:S(2)}, u32[]{:S(2)}) collective-permute-start(f32[128,256]{0,1:T(8,128)S(1)} %add.37), channel_id=1, source_target_pairs={{0,4},{1,5},{2,6},{3,7},{4,0},{5,1},{6,2},{7,3},{8,12},{9,13},{10,... | collective-permute-start | bytes 393224 | tf_op jit(solution)/shard_map/ppermute | solution.py:107
  71.3 5.0 %collective-permute-start.3 = (f32[128,256]{0,1:T(8,128)S(1)}, f32[128,256]{0,1:T(8,128)S(1)}, u32[]{:S(2)}, u32[]{:S(2)}) collective-permute-start(f32[128,256]{0,1:T(8,128)S(1)} %add.38), channel_id=1, source_target_pairs={{0,8},{8,0},{16,24},{24,16},{1,9},{9,1},{17,25},{25,17},{2,10},{10... | collective-permute-start | bytes 393224 | tf_op jit(solution)/shard_map/ppermute | solution.py:107
  71.9 6.5 %collective-permute-start.14 = (f32[128,384]{0,1:T(8,128)S(1)}, f32[128,384]{0,1:T(8,128)S(1)}, u32[]{:S(2)}, u32[]{:S(2)}) collective-permute-start(f32[128,384]{0,1:T(8,128)S(1)} %add.42), channel_id=1, source_target_pairs={{0,2},{1,3},{2,0},{3,1},{4,6},{5,7},{6,4},{7,5},{8,10},{9,11},{10,... | collective-permute-start | bytes 589832 | tf_op jit(solution)/shard_map/ppermute | solution.py:107
  76.3 5.0 %collective-permute-start.4 = (f32[128,256]{0,1:T(8,128)S(1)}, f32[128,256]{0,1:T(8,128)S(1)}, u32[]{:S(2)}, u32[]{:S(2)}) collective-permute-start(f32[128,256]{0,1:T(8,128)S(1)} %add.39), channel_id=1, source_target_pairs={{0,16},{8,24},{16,0},{24,8},{1,17},{9,25},{17,1},{25,9},{2,18},{10... | collective-permute-start | bytes 393224 | tf_op jit(solution)/shard_map/ppermute | solution.py:107
  78.4 18.9 %collective-permute-start.15 = (f32[128,384]{0,1:T(8,128)S(1)}, f32[128,384]{0,1:T(8,128)S(1)}, u32[]{:S(2)}, u32[]{:S(2)}) collective-permute-start(f32[128,384]{0,1:T(8,128)S(1)} %add.43), channel_id=1, source_target_pairs={{0,4},{1,5},{2,6},{3,7},{4,0},{5,1},{6,2},{7,3},{8,12},{9,13},{10,... | collective-permute-start | bytes 589832 | tf_op jit(solution)/shard_map/ppermute | solution.py:107
  97.4 7.8 %copy-start.5 = (f32[128,128]{1,0:T(8,128)S(1)}, f32[128,128]{1,0:T(8,128)}, u32[]{:S(2)}) copy-start(f32[128,128]{1,0:T(8,128)} %shard_map.68) | copy-start | bytes 196612
  97.4 5.7 %collective-permute-start.16 = (f32[128,384]{0,1:T(8,128)S(1)}, f32[128,384]{0,1:T(8,128)S(1)}, u32[]{:S(2)}, u32[]{:S(2)}) collective-permute-start(f32[128,384]{0,1:T(8,128)S(1)} %add.44), channel_id=1, source_target_pairs={{0,8},{8,0},{16,24},{24,16},{1,9},{9,1},{17,25},{25,17},{2,10},{10... | collective-permute-start | bytes 589832 | tf_op jit(solution)/shard_map/ppermute | solution.py:107
  103.2 5.7 %collective-permute-start.17 = (f32[128,384]{0,1:T(8,128)S(1)}, f32[128,384]{0,1:T(8,128)S(1)}, u32[]{:S(2)}, u32[]{:S(2)}) collective-permute-start(f32[128,384]{0,1:T(8,128)S(1)} %add.45), channel_id=1, source_target_pairs={{0,16},{8,24},{16,0},{24,8},{1,17},{9,25},{17,1},{25,9},{2,18},{10... | collective-permute-start | bytes 589832 | tf_op jit(solution)/shard_map/ppermute | solution.py:107
  125.7 3.6 %copy-start.6 = (f32[128,128]{1,0:T(8,128)S(1)}, f32[128,128]{1,0:T(8,128)}, u32[]{:S(2)}) copy-start(f32[128,128]{1,0:T(8,128)} %shard_map.72) | copy-start | bytes 196612
